TPU v7x, 256 devices: a whole 4x4x8 slice. The times are simulated.
256 devices in a mesh: clip: 4 (over z_lo), frame: 16 (over x, y), mp: 4 (over z_hi, core).
Axes of the slice: x: 4, y: 4, z: 8 (z_hi: 2, z_lo: 4; z = z_hi * 4 + z_lo), core: 2. Of those that a mesh axis runs over, the one named last changes fastest.
Arguments:
- query_spatial: bfloat16 [4, 16, 16, 40, 2560], P('clip', 'frame', None, None, 'mp'), may hold values from -24 to 24
- key_spatial: bfloat16 [4, 16, 16, 40, 2560], P('clip', 'frame', None, None, 'mp'), may hold values from -24 to 24
- value_spatial: bfloat16 [4, 16, 16, 40, 2560], P('clip', 'frame', None, None, 'mp'), may hold values from -10 to 10
- gains: float32 [3, 2560], P(None, 'mp'), may hold values from 0.5 to 2.5
- warp_lists: int32 [4, 16, 16], P('clip', 'frame'), may hold values from 0 to 15
- cotangent: bfloat16 [4, 16, 16, 40, 2560], P('clip', None, 'frame', None, 'mp'), may hold values from -3 to 3
Outputs:
- temporal_out: bfloat16 [4, 16, 16, 40, 2560], P('clip', None, 'frame', None, 'mp')
- grad_query: bfloat16 [4, 16, 16, 40, 2560], P('clip', 'frame', None, None, 'mp')
- grad_key: bfloat16 [4, 16, 16, 40, 2560], P('clip', 'frame', None, None, 'mp')
- grad_value: bfloat16 [4, 16, 16, 40, 2560], P('clip', 'frame', None, None, 'mp')
- grad_gains: float32 [3, 2560], P(None, 'mp')
All inputs are finite; a program needn't handle non-finite values.
Results may differ from a plain program's by a relative error of at most 0.035.
Values may be sent and summed in bfloat16 or wider, within the bound.
No kernel may reach another device: no remote copies, remote signals or barrier semaphores. Data moves between devices by JAX's collectives and lax.ppermute only.
A program may use at most 128 MiB of HBM per device.

v0:
```python
import functools
import math

import jax
import jax.numpy as jnp
from jax import lax
from jax.experimental import pallas as pl
from jax.experimental.pallas import tpu as pltpu
from jax.sharding import PartitionSpec as P

HEADS = 20
HD = 128
TILES = 16
TT = 40
TOK = TILES * TT
WIDTH = HEADS * HD
EPS = 1e-06
SCALE = 1.0 / math.sqrt(HD)
LOG2E = math.log2(math.e)
RB = 128
F32 = jnp.float32
BF16 = jnp.bfloat16


def dot_nt(a, b):
    return lax.dot_general(a, b, (((1,), (1,)), ((), ())), preferred_element_type=F32)


def dot_nn(a, b):
    return lax.dot_general(a, b, (((1,), (0,)), ((), ())), preferred_element_type=F32)


def row_sums(x):
    ones = jnp.ones((8, x.shape[1]), F32)
    return lax.dot_general(
        ones, x, (((1,), (1,)), ((), ())), preferred_element_type=F32, precision=lax.Precision.HIGHEST
    )


def as_column(row):
    tall = jnp.broadcast_to(row[0:1, :], (128, row.shape[1]))
    return tall.T


def per_block(x, blocks):
    return jnp.concatenate([x] * blocks, axis=1)


def spatial_forward(q_ref, k_ref, v_ref, o_ref, p_ref, ss_ref, vaug):
    vaug[:, :HD] = v_ref[...]
    vaug[:, HD:] = jnp.ones((TOK, HD), BF16)
    k = k_ref[...]
    for i in range(TOK // RB):
        rows = slice(i * RB, (i + 1) * RB)
        s = dot_nt(q_ref[rows, :], k)
        top = jnp.max(s, axis=-1, keepdims=True)
        e = jnp.exp2((s - top) * (SCALE * LOG2E))
        both = dot_nn(e.astype(BF16), vaug[...])
        inv = 1.0 / both[:, HD:]
        p_ref[0, rows, :] = (e * per_block(inv, TOK // HD)).astype(BF16)
        o = (both[:, :HD] * inv).astype(BF16)
        o_ref[rows, :] = o
        of = o.astype(F32)
        part = row_sums(of * of)

        @pl.when(pl.program_id(0) == 0)
        def _():
            ss_ref[:, rows] = part

        @pl.when(pl.program_id(0) > 0)
        def _():
            ss_ref[:, rows] += part


def pack_normed(warp, sp_ref, ss_ref, send_ref, n_ref):
    inv = lax.rsqrt(as_column(ss_ref[...]) / WIDTH + EPS)
    heads = sp_ref.shape[2] // HD
    for j in range(TILES):
        scaled = sp_ref[j].astype(F32) * per_block(inv[j * TT : (j + 1) * TT], heads)
        normed = scaled.astype(BF16)
        n_ref[j] = normed
        send_ref[j, 0] = normed
    for j in range(TILES):
        send_ref[j, 1] = n_ref[warp[j]]


def temporal(rc_ref, g_ref, gain_ref, out_ref, send_ref, terms_ref, qs, ks, vaug, gs, es, ts, ds):
    gq, gk, gv = gain_ref[0:1, :], gain_ref[1:2, :], gain_ref[2:3, :]
    normed = rc_ref[:, 0].astype(F32).reshape(TOK, HD)
    warped = rc_ref[:, 1].astype(F32).reshape(TOK, HD)
    qs[...] = (normed * gq).astype(BF16)
    ks[...] = (warped * gk).astype(BF16)
    vaug[:, :HD] = (warped * gv).astype(BF16)
    vaug[:, HD:] = jnp.ones((TOK, HD), BF16)
    k = ks[...]
    for i in range(TOK // RB):
        rows = slice(i * RB, (i + 1) * RB)
        q = qs[rows, :]
        g = g_ref[rows, :]
        s = dot_nt(q, k)
        row = lax.broadcasted_iota(jnp.int32, (RB, 1), 0) + i * RB
        limit = (lax.div(row, TT) + 1) * TT
        col = lax.broadcasted_iota(jnp.int32, (RB, TOK), 1)
        s = jnp.where(col < limit, s, -1e30)
        top = jnp.max(s, axis=-1, keepdims=True)
        e = jnp.exp2((s - top) * (SCALE * LOG2E))
        eb = e.astype(BF16)
        both = dot_nn(eb, vaug[...])
        inv = 1.0 / both[:, HD:]
        o = both[:, :HD] * inv
        out_ref[rows, :] = o.astype(BF16)
        gf = g.astype(F32)
        inner = jnp.sum(gf * o, axis=-1, keepdims=True)
        dp = dot_nt(g, vaug[:, :HD])
        t = (e * (dp - inner)).astype(BF16)
        es[rows, :] = eb
        ts[rows, :] = t
        ds[rows, :] = (dot_nn(t, k) * (inv * SCALE)).astype(BF16)
        gs[rows, :] = gf * inv
        qs[rows, :] = (q.astype(F32) * (inv * SCALE)).astype(BF16)
    dk = dot_nn(qs[...].T, ts[...]).T.astype(BF16).astype(F32)
    dv = dot_nn(gs[...].T.astype(BF16), es[...]).T.astype(BF16).astype(F32)
    dq = ds[...].astype(F32)
    send_ref[:, 0] = (dq * gq).reshape(TILES, TT, HD).astype(BF16)
    send_ref[:, 1] = (dk * gk + dv * gv).reshape(TILES, TT, HD).astype(BF16)
    terms_ref[0:1, :] = jnp.sum(dq * normed, axis=0, keepdims=True)
    terms_ref[1:2, :] = jnp.sum(dk * warped, axis=0, keepdims=True)
    terms_ref[2:3, :] = jnp.sum(dv * warped, axis=0, keepdims=True)


def gather_back(warp, rc_ref, sp_ref, gn_ref, in_ref):
    for j in range(TILES):
        gn_ref[j] = rc_ref[j, 0].astype(F32)
    for j in range(TILES):
        gn_ref[warp[j]] += rc_ref[j, 1].astype(F32)
    prod = gn_ref[...] * sp_ref[...].astype(F32)
    in_ref[...] = row_sums(prod.reshape(TOK, sp_ref.shape[2]))


def spatial_backward(
    q_ref, k_ref, v_ref, p_ref, sp_ref, gn_ref, ss_ref, in_ref, dq_ref, dk_ref, dv_ref, gb, ts
):
    inv = lax.rsqrt(as_column(ss_ref[...]) / WIDTH + EPS)
    shift = inv * inv * inv * (as_column(in_ref[...]) / WIDTH)
    spatial = sp_ref[...].astype(F32)
    grad = inv * gn_ref[...] - spatial * shift
    gb[...] = grad
    for i in range(TOK // RB):
        rows = slice(i * RB, (i + 1) * RB)
        g = gb[rows, :].astype(BF16)
        inner = jnp.sum(g.astype(F32) * sp_ref[rows, :].astype(F32), axis=-1, keepdims=True)
        dp = dot_nt(g, v_ref[...])
        t = (p_ref[0, rows, :].astype(F32) * (dp - inner)).astype(BF16)
        ts[rows, :] = t
        dq_ref[rows, :] = (dot_nn(t, k_ref[...]) * SCALE).astype(BF16)
    dk_ref[...] = (dot_nn(q_ref[...].T, ts[...]).T * SCALE).astype(BF16)
    dv_ref[...] = dot_nn(gb[...].T.astype(BF16), p_ref[0]).T.astype(BF16)


def whole(shape):
    return pl.BlockSpec(shape, lambda *_: (0,) * len(shape))


def head_columns():
    return pl.BlockSpec((TOK, HD), lambda h, *_: (0, h))


def params():
    return pltpu.CompilerParams(vmem_limit_bytes=50 * 1024 * 1024)


def summed_over_mp(x):
    x = x + lax.ppermute(x, "mp", [(i, i ^ 1) for i in range(4)])
    return x + lax.ppermute(x, "mp", [(i, i ^ 2) for i in range(4)])


def body(query_spatial, key_spatial, value_spatial, gains, warp_lists, cotangent):
    width = query_spatial.shape[4]
    heads = width // HD
    frame_shape = query_spatial.shape
    tile_shape = cotangent.shape
    q = query_spatial.reshape(TOK, width)
    k = key_spatial.reshape(TOK, width)
    v = value_spatial.reshape(TOK, width)
    g = cotangent.reshape(TOK, width)
    warp = warp_lists[0, 0]
    sds = jax.ShapeDtypeStruct

    spatial, probs, squares = pl.pallas_call(
        spatial_forward,
        grid=(heads,),
        in_specs=[head_columns()] * 3,
        out_specs=[
            head_columns(),
            pl.BlockSpec((1, TOK, TOK), lambda h: (h, 0, 0)),
            whole((8, TOK)),
        ],
        out_shape=[sds((TOK, width), BF16), sds((heads, TOK, TOK), BF16), sds((8, TOK), F32)],
        scratch_shapes=[pltpu.VMEM((TOK, 2 * HD), BF16)],
        compiler_params=params(),
        name="spatial_forward",
    )(q, k, v)
    squares = summed_over_mp(squares)
    spatial3 = spatial.reshape(TILES, TT, width)

    send = pl.pallas_call(
        pack_normed,
        grid_spec=pltpu.PrefetchScalarGridSpec(
            num_scalar_prefetch=1,
            grid=(1,),
            in_specs=[whole((TILES, TT, width)), whole((8, TOK))],
            out_specs=whole((TILES, 2, TT, width)),
            scratch_shapes=[pltpu.VMEM((TILES, TT, width), BF16)],
        ),
        out_shape=sds((TILES, 2, TT, width), BF16),
        compiler_params=params(),
        name="pack_normed",
    )(warp, spatial3, squares)
    got = lax.all_to_all(send, "frame", 0, 0, tiled=True)

    per_head = pl.BlockSpec((TILES, 2, TT, HD), lambda h: (0, 0, 0, h))
    big = pltpu.VMEM((TOK, TOK), BF16)
    out, back, terms = pl.pallas_call(
        temporal,
        grid=(heads,),
        in_specs=[per_head, head_columns(), pl.BlockSpec((3, HD), lambda h: (0, h))],
        out_specs=[head_columns(), per_head, pl.BlockSpec((3, HD), lambda h: (0, h))],
        out_shape=[
            sds((TOK, width), BF16),
            sds((TILES, 2, TT, width), BF16),
            sds((3, width), F32),
        ],
        scratch_shapes=[
            pltpu.VMEM((TOK, HD), BF16),
            pltpu.VMEM((TOK, HD), BF16),
            pltpu.VMEM((TOK, 2 * HD), BF16),
            pltpu.VMEM((TOK, HD), F32),
            big,
            big,
            pltpu.VMEM((TOK, HD), BF16),
        ],
        compiler_params=params(),
        name="temporal",
    )(got, g, gains)
    came = lax.all_to_all(back, "frame", 0, 0, tiled=True)
    everyone = jnp.broadcast_to(terms[None], (64, *terms.shape))
    grad_gains = lax.all_to_all(everyone, ("clip", "frame"), 0, 0, tiled=True).sum(axis=0)

    grad_normed, inner = pl.pallas_call(
        gather_back,
        grid_spec=pltpu.PrefetchScalarGridSpec(
            num_scalar_prefetch=1,
            grid=(1,),
            in_specs=[whole((TILES, 2, TT, width)), whole((TILES, TT, width))],
            out_specs=[whole((TILES, TT, width)), whole((8, TOK))],
        ),
        out_shape=[sds((TILES, TT, width), F32), sds((8, TOK), F32)],
        compiler_params=params(),
        name="gather_back",
    )(warp, came, spatial3)
    inner = summed_over_mp(inner)

    dq, dk, dv = pl.pallas_call(
        spatial_backward,
        grid=(heads,),
        in_specs=[head_columns()] * 3
        + [pl.BlockSpec((1, TOK, TOK), lambda h: (h, 0, 0))]
        + [head_columns()] * 2
        + [whole((8, TOK))] * 2,
        out_specs=[head_columns()] * 3,
        out_shape=[sds((TOK, width), BF16)] * 3,
        scratch_shapes=[pltpu.VMEM((TOK, HD), F32), big],
        compiler_params=params(),
        name="spatial_backward",
    )(q, k, v, probs, spatial, grad_normed.reshape(TOK, width), squares, inner)
    return (
        out.reshape(tile_shape),
        dq.reshape(frame_shape),
        dk.reshape(frame_shape),
        dv.reshape(frame_shape),
        grad_gains,
    )


def solution(mesh):
    frames = P("clip", "frame", None, None, "mp")
    tiles = P("clip", None, "frame", None, "mp")
    return jax.shard_map(
        body,
        mesh=mesh,
        in_specs=(frames, frames, frames, P(None, "mp"), P("clip", "frame", None), tiles),
        out_specs=(tiles, frames, frames, frames, P(None, "mp")),
        check_vma=False,
    )
```

profile of v0, /device:TPU:8, one launch (start us, length us, event | category | flops | bytes accessed | tf_op | source)
XLA Modules:
  0.0 151.1 jit_solution(4828328559714449433)
XLA Ops:
  0.6 0.0 copy-start.9
  0.6 0.0 copy-start
  0.7 1.1 copy-done
  1.8 0.0 copy-start.2
  1.8 1.1 copy-done.2
  2.9 0.0 copy-start.4
  2.9 1.1 copy-done.4
  4.1 22.1 %spatial_forward.1 = (bf16[640,640]{1,0:T(8,128)(2,1)S(1)}, bf16[5,640,640]{2,1,0:T(8,128)(2,1)}, f32[8,640]{1,0:T(8,128)S(1)}) custom-call(bf16[640,640]{1,0:T(8,128)(2,1)S(1)} %bitcast.15, bf16[640,640]{1,0:T(8,128)(2,1)S(1)} %bitcast.17, bf16[640,640]{1,0:T(8,128)(2,1)S(1)} %bitcast.19), custom_call_target="tpu_custom_call" | custom-call | tf_op jit(solution)/shard_map/spatial_forward/pallas_call | solution.py:189
  26.1 0.0 collective-permute-start
  26.2 1.2 collective-permute-done
  27.3 7.2 %collective-permute-start.1 = (f32[8,640]{1,0:T(8,128)S(1)}, f32[8,640]{1,0:T(8,128)S(1)}, u32[]{:S(2)}, u32[]{:S(2)}) collective-permute-start(f32[8,640]{1,0:T(8,128)S(1)} %add.12), channel_id=1, source_target_pairs={{0,2},{1,3},{2,0},{3,1},{4,6},{5,7},{6,4},{7,5},{8,10},{9,11},{10,... | collective-permute-start | bytes 61448 | tf_op jit(solution)/shard_map/ppermute | solution.py:174
  34.5 1.8 %collective-permute-done.1 = f32[8,640]{1,0:T(8,128)S(1)} collective-permute-done((f32[8,640]{1,0:T(8,128)S(1)}, f32[8,640]{1,0:T(8,128)S(1)}, u32[]{:S(2)}, u32[]{:S(2)}) %collective-permute-start.1) | collective-permute-done | bytes 20512 | tf_op jit(solution)/shard_map/ppermute | solution.py:174
  36.3 0.0 copy-done.9
  36.3 0.8 pack_normed.1
  37.2 0.0 copy-start.7
  37.2 0.0 copy-start.8
  37.2 28.9 %all_to_all.15.rc_ref = bf16[16,2,40,640]{3,2,1,0:T(8,128)(2,1)S(1)} all-to-all(bf16[16,2,40,640]{3,2,1,0:T(8,128)(2,1)S(1)} %pack_normed.1), channel_id=1, replica_groups=mesh['clip'=4,'frame'=16,'mp'=4] {'frame'}, dimensions={0} | all-to-all | bytes 3276800 | tf_op jit(solution)/shard_map/all_to_all | solution.py:219
  66.1 0.0 copy-done.7
  66.1 0.0 copy-done.8
  66.1 19.0 %temporal.1 = (bf16[640,640]{1,0:T(8,128)(2,1)}, bf16[16,2,40,640]{3,2,1,0:T(8,128)(2,1)S(1)}, f32[3,640]{1,0:T(4,128)S(1)}) custom-call(bf16[16,2,40,640]{3,2,1,0:T(8,128)(2,1)S(1)} %all_to_all.15.rc_ref, bf16[640,640]{1,0:T(8,128)(2,1)S(1)} %bitcast.22, f32[3,640]{1,0:T(4,128)S(1)} %copy-done.8), custom_call_target="tpu_custom_call" | custom-call | tf_op jit(solution)/shard_map/temporal/pallas_call | solution.py:223
  85.0 25.3 %all_to_all.16.rc_ref = bf16[16,2,40,640]{3,2,1,0:T(8,128)(2,1)S(1)} all-to-all(bf16[16,2,40,640]{3,2,1,0:T(8,128)(2,1)S(1)} %get-tuple-element.20), channel_id=1, replica_groups=mesh['clip'=4,'frame'=16,'mp'=4] {'frame'}, dimensions={0} | all-to-all | bytes 3276800 | tf_op jit(solution)/shard_map/all_to_all | solution.py:245
  110.3 0.9 broadcast_in_dim.2
  111.2 8.0 %all-to-all-start.2 = ((f32[64,3,640]{2,1,0:T(4,128)}), f32[64,3,640]{2,1,0:T(4,128)}, u32[]{:S(2)}, u32[]{:S(2)}) async-start(f32[64,3,640]{2,1,0:T(4,128)} %broadcast_in_dim.2), calls=%async_computation.2 | async-start | bytes 1310720 | tf_op jit(solution)/shard_map/all_to_all | solution.py:247
  119.2 0.0 copy-start.1
  119.2 2.3 %gather_back.1 = (f32[16,40,640]{2,1,0:T(8,128)S(1)}, f32[8,640]{1,0:T(8,128)S(1)}) custom-call(s32[16]{0:T(128)S(1)} %bitcast.24, bf16[16,2,40,640]{3,2,1,0:T(8,128)(2,1)S(1)} %all_to_all.16.rc_ref, bf16[16,40,640]{2,1,0:T(8,128)(2,1)S(1)} %bitcast.14), custom_call_target="tpu_custom_call" | custom-call | tf_op jit(solution)/shard_map/gather_back/pallas_call | solution.py:249
  121.5 0.0 copy-start.6
  121.5 1.2 copy-done.6
  122.7 0.0 collective-permute-start.2
  122.8 1.2 collective-permute-done.2
  123.9 4.7 %collective-permute-start.3 = (f32[8,640]{1,0:T(8,128)S(1)}, f32[8,640]{1,0:T(8,128)S(1)}, u32[]{:S(2)}, u32[]{:S(2)}) collective-permute-start(f32[8,640]{1,0:T(8,128)S(1)} %add.14), channel_id=1, source_target_pairs={{0,2},{1,3},{2,0},{3,1},{4,6},{5,7},{6,4},{7,5},{8,10},{9,11},{10,... | collective-permute-start | bytes 61448 | tf_op jit(solution)/shard_map/ppermute | solution.py:174
  128.7 8.0 %all-to-all-done.2 = f32[64,3,640]{2,1,0:T(4,128)} async-done(((f32[64,3,640]{2,1,0:T(4,128)}), f32[64,3,640]{2,1,0:T(4,128)}, u32[]{:S(2)}, u32[]{:S(2)}) %all-to-all-start.2) | async-done | bytes 491552 | tf_op jit(solution)/shard_map/all_to_all | solution.py:247
  136.7 1.8 %reduce_sum.9 = f32[3,640]{1,0:T(4,128)} reduce(f32[64,3,640]{2,1,0:T(4,128)} %all-to-all-done.2, f32[]{:T(128)} %constant.0.clone.1), dimensions={0}, to_apply=%region_0.0 | reduce | flops 120960 | bytes 499204 | tf_op jit(solution)/shard_map/reduce_sum | solution.py:247
  138.5 0.0 collective-permute-done.3
  138.5 0.0 copy-done.1
  138.5 0.0 copy-start.3
  138.5 1.1 copy-done.3
  139.7 0.0 copy-start.5
  139.7 1.1 copy-done.5
  140.8 10.3 %spatial_backward.1 = (bf16[640,640]{1,0:T(8,128)(2,1)}, bf16[640,640]{1,0:T(8,128)(2,1)}, bf16[640,640]{1,0:T(8,128)(2,1)}) custom-call(bf16[640,640]{1,0:T(8,128)(2,1)S(1)} %bitcast.16, bf16[640,640]{1,0:T(8,128)(2,1)S(1)} %bitcast.18, bf16[640,640]{1,0:T(8,128)(2,1)S(1)} %bitcast.20, bf16[5,640,640]{2,1,0:T(8,128)(2,1)} %get-tuple-element.19.p_ref, ...), custom_call_target="tpu_custom_call" | custom-call | tf_op jit(solution)/shard_map/spatial_backward/pallas_call | solution.py:263
  (4 shorter events, 0.0 us)
Async XLA Ops:
  0.6 35.7 %copy-start.9 = (s32[1,1,16]{2,1,0:T(1,128)S(1)}, s32[1,1,16]{2,1,0:T(1,128)}, u32[]{:S(2)}) copy-start(s32[1,1,16]{2,1,0:T(1,128)} %param.10) | copy-start | bytes 196
  0.6 1.2 copy-start
  1.8 1.1 copy-start.2
  2.9 1.1 copy-start.4
  26.1 1.2 collective-permute-start
  27.3 9.0 %collective-permute-start.1 = (f32[8,640]{1,0:T(8,128)S(1)}, f32[8,640]{1,0:T(8,128)S(1)}, u32[]{:S(2)}, u32[]{:S(2)}) collective-permute-start(f32[8,640]{1,0:T(8,128)S(1)} %add.12), channel_id=1, source_target_pairs={{0,2},{1,3},{2,0},{3,1},{4,6},{5,7},{6,4},{7,5},{8,10},{9,11},{10,... | collective-permute-start | bytes 61448 | tf_op jit(solution)/shard_map/ppermute | solution.py:174
  37.2 28.9 %copy-start.7 = (bf16[1,16,1,40,640]{4,3,2,1,0:T(8,128)(2,1)S(1)}, bf16[1,16,1,40,640]{4,3,2,1,0:T(8,128)(2,1)}, u32[]{:S(2)}) copy-start(bf16[1,16,1,40,640]{4,3,2,1,0:T(8,128)(2,1)} %param.11) | copy-start | bytes 2457604
  37.2 28.9 %copy-start.8 = (f32[3,640]{1,0:T(4,128)S(1)}, f32[3,640]{1,0:T(4,128)}, u32[]{:S(2)}) copy-start(f32[3,640]{1,0:T(4,128)} %gain_ref.1) | copy-start | bytes 23044
  111.2 25.4 %all-to-all-start.2 = ((f32[64,3,640]{2,1,0:T(4,128)}), f32[64,3,640]{2,1,0:T(4,128)}, u32[]{:S(2)}, u32[]{:S(2)}) async-start(f32[64,3,640]{2,1,0:T(4,128)} %broadcast_in_dim.2), calls=%async_computation.2 | async-start | bytes 1310720 | tf_op jit(solution)/shard_map/all_to_all | solution.py:247
  119.2 19.3 %copy-start.1 = (bf16[1,1,16,40,640]{4,3,2,1,0:T(8,128)(2,1)S(1)}, bf16[1,1,16,40,640]{4,3,2,1,0:T(8,128)(2,1)}, u32[]{:S(2)}) copy-start(bf16[1,1,16,40,640]{4,3,2,1,0:T(8,128)(2,1)} %param.6) | copy-start | bytes 2457604
  121.5 1.2 copy-start.6
  122.7 1.2 collective-permute-start.2
  123.9 14.6 %collective-permute-start.3 = (f32[8,640]{1,0:T(8,128)S(1)}, f32[8,640]{1,0:T(8,128)S(1)}, u32[]{:S(2)}, u32[]{:S(2)}) collective-permute-start(f32[8,640]{1,0:T(8,128)S(1)} %add.14), channel_id=1, source_target_pairs={{0,2},{1,3},{2,0},{3,1},{4,6},{5,7},{6,4},{7,5},{8,10},{9,11},{10,... | collective-permute-start | bytes 61448 | tf_op jit(solution)/shard_map/ppermute | solution.py:174
  138.5 1.1 copy-start.3
  139.7 1.1 copy-start.5
where the time goes:
time: 152 us; the launch traced here: 151 us
  Pallas kernels  54.5 us (36%)
  blocking collectives  54.2 us (36%)
  starting transfers between devices  19.9 us (13%)
  waiting for transfers between devices  12.2 us (8%)
  local copies, waits for them, and re-layouts  7.88 us (5%)
  other arithmetic  1.83 us (1%)
    all_to_all x1, blocking collectives, body(): got = lax.all_to_all(send, 'frame', 0, 0, tiled=True)  28.9 us
    all_to_all x1, blocking collectives, body(): came = lax.all_to_all(back, 'frame', 0, 0, tiled=True)  25.3 us
    pallas_call x1, Pallas kernels, body(): pl.pallas_call(spatial_forward, grid=(heads,), in_specs=[head_columns()]...  22.1 us
    pallas_call x1, Pallas kernels, body(): pl.pallas_call(temporal, grid=(heads,), in_specs=[per_head, head_columns(...  19 us
    ppermute x2, starting transfers between devices, summed_over_mp(): return x + lax.ppermute(x, 'mp', [(i, i ^ 2) for i in range(4)])  11.9 us
    pallas_call x1, Pallas kernels, body(): pl.pallas_call(spatial_backward, grid=(heads,), in_specs=[head_columns()]...  10.3 us
    all_to_all x1, waiting for transfers between devices, body(): lax.all_to_all(everyone, ('clip', 'frame'), 0, 0, tiled=True).sum(axis=0)  8.02 us
    all_to_all x1, starting transfers between devices, body(): lax.all_to_all(everyone, ('clip', 'frame'), 0, 0, tiled=True).sum(axis=0)  7.97 us
  transfers between devices with their start and end apart: 5, of which 4 were waited for; matrix products, arithmetic and copies ran while one was open for 1% of the time, Pallas kernels for 2%

commit v1 on v0

v1 whole, which is shorter than its diff:
```python
import math

import jax
import jax.numpy as jnp
from jax import lax
from jax.experimental import pallas as pl
from jax.experimental.pallas import tpu as pltpu
from jax.sharding import PartitionSpec as P


HEADS = 20
HD = 128
TILES = 16
TT = 40
TOK = TILES * TT
WIDTH = HEADS * HD
HERE = 5
EPS = 1e-06
SCALE = 1.0 / math.sqrt(HD)
LOG2E = math.log2(math.e)
RB = 128
BLOCKS = TOK // RB
F32 = jnp.float32
BF16 = jnp.bfloat16


def dot_nt(a, b):
    return lax.dot_general(a, b, (((1,), (1,)), ((), ())), preferred_element_type=F32)


def dot_nn(a, b):
    return lax.dot_general(a, b, (((1,), (0,)), ((), ())), preferred_element_type=F32)


def row_sums(x):
    ones = jnp.ones((8, x.shape[1]), F32)
    return lax.dot_general(
        ones, x, (((1,), (1,)), ((), ())), preferred_element_type=F32, precision=lax.Precision.HIGHEST
    )


def column_sum(x):
    x = jnp.sum(x.reshape(10, 64, HD), axis=0)
    return jnp.sum(x, axis=0, keepdims=True)


def as_column(row):
    return jnp.broadcast_to(row, (128, row.shape[1])).T


def softmax_rows(s):
    top = jnp.max(s, axis=-1, keepdims=True)
    e = jnp.exp2((s - top) * (SCALE * LOG2E))
    return (e * (1.0 / jnp.sum(e, axis=-1, keepdims=True))).astype(BF16)


def across(x_t):
    x_t = x_t.astype(BF16)
    r = lax.broadcasted_iota(jnp.int32, (HD, HD), 0)
    c = lax.broadcasted_iota(jnp.int32, (HD, HD), 1)
    eye = jnp.where(r == c, 1.0, 0.0).astype(BF16)
    parts = [dot_nt(eye, x_t[:, i : i + HD]) for i in range(0, x_t.shape[1], HD)]
    return jnp.concatenate(parts, axis=0)


def spatial_forward(q_ref, k_ref, v_ref, o_ref, p_ref, ss_ref, acc):
    h = pl.program_id(0)

    @pl.when(h == 0)
    def _():
        acc[...] = jnp.zeros_like(acc)

    k = k_ref[...]
    v = v_ref[...]
    for i in range(BLOCKS):
        rows = slice(i * RB, (i + 1) * RB)
        p = softmax_rows(dot_nt(q_ref[rows, :], k))
        p_ref[0, rows, :] = p
        o = dot_nn(p, v).astype(BF16)
        o_ref[rows, :] = o
        of = o.astype(F32)
        acc[rows, :] += of * of

    @pl.when(h == pl.num_programs(0) - 1)
    def _():
        ss_ref[...] = row_sums(acc[...])[0:1]


def pack_normed(warp, sp_ref, one_ref, two_ref, send_ref, inv_ref, n_ref):
    @pl.when(pl.program_id(0) == 0)
    def _():
        inv = lax.rsqrt((one_ref[...] + two_ref[...]) / WIDTH + EPS)
        inv_ref[...] = as_column(inv).reshape(TILES, TT, HD)

    normed = (sp_ref[...].astype(F32) * inv_ref[...]).astype(BF16)
    n_ref[...] = normed
    send_ref[:, 0] = normed
    for j in range(TILES):
        send_ref[j, 1] = n_ref[warp[j]]


def temporal(
    rc_ref, g_ref, gain_ref, out_ref, send_ref, terms_ref, qs, ks, vs, ps, ts, ds
):
    h = pl.program_id(0)

    @pl.when(h == 0)
    def _():
        ps[...] = jnp.zeros_like(ps)
        ts[...] = jnp.zeros_like(ts)

    gq, gk, gv = gain_ref[0:1, :], gain_ref[1:2, :], gain_ref[2:3, :]
    normed = rc_ref[:, 0].astype(F32).reshape(TOK, HD)
    warped = rc_ref[:, 1].astype(F32).reshape(TOK, HD)
    qs[...] = (normed * gq).astype(BF16)
    ks[...] = (warped * gk).astype(BF16)
    vs[...] = (warped * gv).astype(BF16)
    for i in range(BLOCKS):
        rows = slice(i * RB, (i + 1) * RB)
        last = ((i * RB + RB - 1) // TT + 1) * TT
        keys = max(min(-(-last // HD) * HD, TOK), 2 * HD)
        clear = ((i * RB) // TT + 1) * TT // HD * HD
        g = g_ref[rows, :]
        k = ks[:keys, :]
        v = vs[:keys, :]
        s = dot_nt(qs[rows, :], k)
        row = lax.broadcasted_iota(jnp.int32, (RB, 1), 0).astype(F32) + (i * RB + 0.5)
        limit = (jnp.floor(row * (1.0 / TT)) + 1.0) * TT
        col = lax.broadcasted_iota(jnp.int32, (RB, keys - clear), 1).astype(F32) + clear
        masked = jnp.where(col < limit, s[:, clear:], -1e30)
        s = jnp.concatenate([s[:, :clear], masked], axis=1) if clear else masked
        p = softmax_rows(s)
        ps[rows, :keys] = p
        o = dot_nn(p, v)
        out_ref[rows, :] = o.astype(BF16)
        inner = jnp.sum(g.astype(F32) * o, axis=-1, keepdims=True)
        t = p * (dot_nt(g, v) - inner).astype(BF16)
        ts[rows, :keys] = t
        ds[rows, :] = dot_nn(t, k) * SCALE

    def by_keys(left, right):
        lt = left[...].T
        parts = [
            dot_nn(lt, right[:, : 2 * HD]),
            dot_nn(lt[:, RB:], right[RB:, 2 * HD : 4 * HD]),
            dot_nn(lt[:, 3 * RB :], right[3 * RB :, 4 * HD :]),
        ]
        return jnp.concatenate([across(x) for x in parts], axis=0)

    dk = by_keys(qs, ts) * SCALE
    dv = by_keys(g_ref, ps)
    dq = ds[...]
    normed = rc_ref[:, 0].astype(F32).reshape(TOK, HD)
    warped = rc_ref[:, 1].astype(F32).reshape(TOK, HD)
    send_ref[:, 0] = (dq * gq).reshape(TILES, TT, HD).astype(BF16)
    send_ref[:, 1] = (dk * gk + dv * gv).reshape(TILES, TT, HD).astype(BF16)
    terms_ref[0:1, :] = column_sum(dq * normed)
    terms_ref[1:2, :] = column_sum(dk * warped)
    terms_ref[2:3, :] = column_sum(dv * warped)


def gather_back(warp, rc_ref, sp_ref, gn_ref, in_ref, acc):
    h = pl.program_id(0)
    gn_ref[...] = rc_ref[:, 0].astype(F32)
    for j in range(TILES):
        gn_ref[warp[j]] += rc_ref[j, 1].astype(F32)
    prod = gn_ref[...] * sp_ref[...].astype(F32)

    @pl.when(h == 0)
    def _():
        acc[...] = prod

    @pl.when(h > 0)
    def _():
        acc[...] += prod

    @pl.when(h == pl.num_programs(0) - 1)
    def _():
        in_ref[...] = row_sums(acc[...].reshape(TOK, HD))[0:1]


def spatial_backward(
    q_ref, k_ref, v_ref, p_ref, sp_ref, gn_ref, s1_ref, s2_ref, i1_ref, i2_ref,
    dq_ref, dk_ref, dv_ref, inv_s, shift, gb, ts,
):
    @pl.when(pl.program_id(0) == 0)
    def _():
        inv = lax.rsqrt((s1_ref[...] + s2_ref[...]) / WIDTH + EPS)
        inv_s[...] = as_column(inv)
        shift[...] = as_column(inv * inv * inv * ((i1_ref[...] + i2_ref[...]) / WIDTH))

    k = k_ref[...]
    v = v_ref[...]
    for i in range(BLOCKS):
        rows = slice(i * RB, (i + 1) * RB)
        spatial = sp_ref[rows, :].astype(F32)
        grad = inv_s[rows, :] * gn_ref[rows, :] - spatial * shift[rows, :]
        g = grad.astype(BF16)
        gb[rows, :] = g
        inner = jnp.sum(g.astype(F32) * spatial, axis=-1, keepdims=True)
        t = p_ref[0, rows, :] * (dot_nt(g, v) - inner).astype(BF16)
        ts[rows, :] = t
        dq_ref[rows, :] = (dot_nn(t, k) * SCALE).astype(BF16)
    dk_ref[...] = across(dot_nn(q_ref[...].T, ts[...]) * SCALE).astype(BF16)
    dv_ref[...] = across(dot_nn(gb[...].T, p_ref[0])).astype(BF16)


def whole(shape):
    return pl.BlockSpec(shape, lambda *_: (0,) * len(shape))


def columns(rows=TOK):
    return pl.BlockSpec((rows, HD), lambda h, *_: (0, h))


def call(kernel, in_specs, out_specs, out_shape, scratch, us, prefetch=0, limit=63):
    return pl.pallas_call(
        kernel,
        grid_spec=pltpu.PrefetchScalarGridSpec(
            num_scalar_prefetch=prefetch,
            grid=(HERE,),
            in_specs=in_specs,
            out_specs=out_specs,
            scratch_shapes=scratch,
        ),
        out_shape=out_shape,
        cost_estimate=pl.CostEstimate(
            flops=int(us * 1e6), bytes_accessed=int(us * 3.0e6), transcendentals=0
        ),
        compiler_params=pltpu.CompilerParams(vmem_limit_bytes=limit * 1024 * 1024),
    )


def swapped(x, axis, flip):
    size = lax.axis_size(axis)
    return lax.ppermute(x, axis, [(i, i ^ flip) for i in range(size)])


def half_sums(x, axis):
    x = x + swapped(x, axis, 1)
    return x, swapped(x, axis, 2)


def exchanged(x):
    return lax.all_to_all(x, "frame", 0, 0, tiled=True)


def body(query_spatial, key_spatial, value_spatial, gains, warp_lists, cotangent):
    width = HERE * HD
    q = query_spatial.reshape(TOK, width)
    k = key_spatial.reshape(TOK, width)
    v = value_spatial.reshape(TOK, width)
    g = cotangent.reshape(TOK, width)
    warp = warp_lists[0, 0]
    sds = jax.ShapeDtypeStruct
    tall = pltpu.VMEM((TOK, HD), F32)
    thin = pltpu.VMEM((TOK, HD), BF16)
    big = pltpu.VMEM((TOK, TOK), BF16)
    cube = pltpu.VMEM((TILES, TT, HD), F32)
    square = pl.BlockSpec((1, TOK, TOK), lambda h, *_: (h, 0, 0))
    tiles = pl.BlockSpec((TILES, TT, HD), lambda h, *_: (0, 0, h))
    pairs = pl.BlockSpec((TILES, 2, TT, HD), lambda h, *_: (0, 0, 0, h))
    line = whole((1, TOK))
    both = sds((TILES, 2, TT, width), BF16)
    flat = sds((TOK, width), BF16)

    spatial, probs, squares = call(
        spatial_forward,
        [columns()] * 3,
        [columns(), square, line],
        [flat, sds((HERE, TOK, TOK), BF16), sds((1, TOK), F32)],
        [tall],
        7,
    )(q, k, v)
    ss_one, ss_two = half_sums(squares, "mp")
    spatial_tiles = spatial.reshape(TILES, TT, width)
    send = call(
        pack_normed,
        [tiles, line, line],
        pairs,
        both,
        [cube, pltpu.VMEM((TILES, TT, HD), BF16)],
        1,
        prefetch=1,
    )(warp, spatial_tiles, ss_one, ss_two)
    got = exchanged(send)

    out, back, terms = call(
        temporal,
        [pairs, columns(), columns(3)],
        [columns(), pairs, columns(3)],
        [flat, both, sds((3, width), F32)],
        [thin, thin, thin, big, big, tall],
        16,
    )(got, g, gains)
    came = exchanged(back)
    for axis, flips in (("clip", (1, 2)), ("frame", (1, 2, 4, 8))):
        for flip in flips:
            terms = terms + swapped(terms, axis, flip)

    grad_normed, inner = call(
        gather_back,
        [pairs, tiles],
        [tiles, line],
        [sds((TILES, TT, width), F32), sds((1, TOK), F32)],
        [cube],
        2,
        prefetch=1,
    )(warp, came, spatial_tiles)
    in_one, in_two = half_sums(inner, "mp")

    dq, dk, dv = call(
        spatial_backward,
        [columns()] * 3 + [square] + [columns()] * 2 + [line] * 4,
        [columns()] * 3,
        [flat] * 3,
        [tall, tall, thin, big],
        9,
    )(q, k, v, probs, spatial, grad_normed.reshape(TOK, width), ss_one, ss_two, in_one, in_two)
    return (
        out.reshape(cotangent.shape),
        dq.reshape(query_spatial.shape),
        dk.reshape(query_spatial.shape),
        dv.reshape(query_spatial.shape),
        terms,
    )


def solution(mesh):
    frames = P("clip", "frame", None, None, "mp")
    tiles = P("clip", None, "frame", None, "mp")
    return jax.shard_map(
        body,
        mesh=mesh,
        in_specs=(frames, frames, frames, P(None, "mp"), P("clip", "frame", None), tiles),
        out_specs=(tiles, frames, frames, frames, P(None, "mp")),
        check_vma=False,
    )
```

time: 152 us -> 144 us (0.947)
  blocking collectives: 54.2 us -> 29 us
  waiting for transfers between devices: 12.2 us -> 25.8 us
  starting transfers between devices: 19.9 us -> 27.4 us
  local copies, waits for them, and re-layouts: 7.88 us -> 1.18 us
  Pallas kernels: 54.5 us -> 56.3 us
    all_to_all x2 -> x1, blocking collectives: 54.2 us -> 29 us  [exchanged(): return lax.all_to_all(x, 'frame', 0, 0, tiled=True)]
    ppermute x4 -> x10, waiting for transfers between devices: 4.14 us -> 25.8 us  [swapped(): return lax.ppermute(x, axis, [(i, i ^ flip) for i in range(size)])]
    ppermute x4 -> x10, starting transfers between devices: 11.9 us -> 21.7 us  [swapped(): return lax.ppermute(x, axis, [(i, i ^ flip) for i in range(size)])]
    all_to_all x1, waiting for transfers between devices: 8.02 us -> 0.01 us  [exchanged(): return lax.all_to_all(x, 'frame', 0, 0, tiled=True)]
    unnamed x20 -> x10, local copies, waits for them, and re-layouts: 6.96 us -> 1.18 us
    all_to_all x1, starting transfers between devices: 7.97 us -> 5.76 us  [exchanged(): return lax.all_to_all(x, 'frame', 0, 0, tiled=True)]
    add x4 -> x8, other arithmetic: 0.02 us -> 2 us  [the longest x2 1.37 us: half_sums(): x = x + swapped(x, axis, 1)]
    reduce_sum x1 -> x0, other arithmetic: 1.81 us -> none  [body(): lax.all_to_all(everyone, ('clip', 'frame'), 0, 0, tiled=True).sum(axis=0)]
  transfers between devices with their start and end apart: 5 -> 11, of which waited for: 4 -> 9; matrix products, arithmetic and copies ran while one was open for 1% -> 1% of each run, Pallas kernels for 2% -> 4%
where the time goes in v1:
time: 144 us; the launch traced here: 142 us
  Pallas kernels  56.3 us (39%)
  blocking collectives  29 us (20%)
  starting transfers between devices  27.4 us (19%)
  waiting for transfers between devices  25.8 us (18%)
  other arithmetic  2 us (1%)
    all_to_all x1, blocking collectives, exchanged(): return lax.all_to_all(x, 'frame', 0, 0, tiled=True)  29 us
    ppermute x10, waiting for transfers between devices, swapped(): return lax.ppermute(x, axis, [(i, i ^ flip) for i in range(size)])  25.8 us
    ppermute x10, starting transfers between devices, swapped(): return lax.ppermute(x, axis, [(i, i ^ flip) for i in range(size)])  21.7 us
    pallas_call x1, Pallas kernels, body(): call(temporal, [pairs, columns(), columns(3)], [columns(), pairs, columns...  20.6 us
    pallas_call x1, Pallas kernels, body(): call(spatial_forward, [columns()] * 3, [columns(), square, line], [flat,...  13.4 us
    pallas_call x1, Pallas kernels, body(): call(spatial_backward, [columns()] * 3 + [square] + [columns()] * 2 + [li...  11.5 us
    pallas_call x1, Pallas kernels, body(): call(gather_back, [pairs, tiles], [tiles, line], [sds((TILES, TT, width),...  5.84 us
    all_to_all x1, starting transfers between devices, exchanged(): return lax.all_to_all(x, 'frame', 0, 0, tiled=True)  5.76 us
  transfers between devices with their start and end apart: 11, of which 9 were waited for; matrix products, arithmetic and copies ran while one was open for 1% of the time, Pallas kernels for 4%

profile of v1, /device:TPU:8, one launch (start us, length us, event | category | flops | bytes accessed | tf_op | source)
XLA Modules:
  0.0 142.4 jit_solution(7923210181527750955)
XLA Ops:
  0.6 13.4 %shard_map.101 = (bf16[640,640]{1,0:T(8,128)(2,1)}, bf16[5,640,640]{2,1,0:T(8,128)(2,1)}, f32[1,640]{1,0:T(1,128)}) custom-call(bf16[640,640]{1,0:T(8,128)(2,1)} %bitcast.15, bf16[640,640]{1,0:T(8,128)(2,1)} %bitcast.17, bf16[640,640]{1,0:T(8,128)(2,1)} %bitcast.19), custom_call_target="tpu_custom_call" | custom-call | flops 7000000 | bytes 21000000 | tf_op jit(solution)/shard_map/pallas_call | solution.py:267
  14.0 0.0 collective-permute-start
  14.1 1.4 collective-permute-done
  15.4 0.7 add.24.one_ref.s1_ref
  16.1 0.0 copy-start
  16.1 7.2 %collective-permute-start.1 = (f32[1,640]{1,0:T(1,128)S(1)}, f32[1,640]{1,0:T(1,128)S(1)}, u32[]{:S(2)}, u32[]{:S(2)}) collective-permute-start(f32[1,640]{1,0:T(1,128)S(1)} %add.24.one_ref.s1_ref), channel_id=1, source_target_pairs={{0,2},{1,3},{2,0},{3,1},{4,6},{5,7},{6,4},{7,5},{8,10},{9,11},{10,... | collective-permute-start | bytes 7688 | tf_op jit(solution)/shard_map/ppermute | solution.py:236
  23.3 1.6 %collective-permute-done.1.two_ref.s2_ref = f32[1,640]{1,0:T(1,128)S(1)} collective-permute-done((f32[1,640]{1,0:T(1,128)S(1)}, f32[1,640]{1,0:T(1,128)S(1)}, u32[]{:S(2)}, u32[]{:S(2)}) %collective-permute-start.1) | collective-permute-done | bytes 2592 | tf_op jit(solution)/shard_map/ppermute | solution.py:236
  24.9 0.0 copy-start.2
  24.9 0.0 copy-done
  24.9 0.6 copy-done.2
  25.4 4.9 %shard_map.102 = bf16[16,2,40,640]{3,2,1,0:T(8,128)(2,1)} custom-call(s32[16]{0:T(128)} %bitcast.23, bf16[16,40,640]{2,1,0:T(8,128)(2,1)} %bitcast.13, f32[1,640]{1,0:T(1,128)} %copy-done, f32[1,640]{1,0:T(1,128)} %copy-done.2), custom_call_target="tpu_custom_call" | custom-call | flops 1000000 | bytes 3000000 | tf_op jit(solution)/shard_map/pallas_call | solution.py:277
  30.4 29.0 %all_to_all.10.rc_ref = bf16[16,2,40,640]{3,2,1,0:T(8,128)(2,1)} all-to-all(bf16[16,2,40,640]{3,2,1,0:T(8,128)(2,1)} %shard_map.102), channel_id=1, replica_groups=mesh['clip'=4,'frame'=16,'mp'=4] {'frame'}, dimensions={0} | all-to-all | bytes 3276800 | tf_op jit(solution)/shard_map/all_to_all | solution.py:245
  59.4 20.6 %shard_map.103 = (bf16[640,640]{1,0:T(8,128)(2,1)}, bf16[16,2,40,640]{3,2,1,0:T(8,128)(2,1)}, f32[3,640]{1,0:T(4,128)}) custom-call(bf16[16,2,40,640]{3,2,1,0:T(8,128)(2,1)} %all_to_all.10.rc_ref, bf16[640,640]{1,0:T(8,128)(2,1)} %bitcast.22, f32[3,640]{1,0:T(4,128)} %gain_ref.1), custom_call_target="tpu_custom_call" | custom-call | flops 16000000 | bytes 48000000 | tf_op jit(solution)/shard_map/pallas_call | solution.py:288
  80.1 0.0 copy-start.1
  80.1 5.8 %all-to-all-start.1 = ((bf16[16,2,40,640]{3,2,1,0:T(8,128)(2,1)}), bf16[16,2,40,640]{3,2,1,0:T(8,128)(2,1)}, u32[]{:S(2)}, u32[]{:S(2)}) async-start(bf16[16,2,40,640]{3,2,1,0:T(8,128)(2,1)} %get-tuple-element.20), calls=%async_computation.1 | async-start | bytes 3276800 | tf_op jit(solution)/shard_map/all_to_all | solution.py:245
  85.8 0.0 copy-done.1
  85.8 1.1 collective-permute-start.4
  86.9 2.7 %collective-permute-done.4 = f32[3,640]{1,0:T(4,128)S(1)} collective-permute-done((f32[3,640]{1,0:T(4,128)S(1)}, f32[3,640]{1,0:T(4,128)S(1)}, u32[]{:S(2)}, u32[]{:S(2)}) %collective-permute-start.4) | collective-permute-done | bytes 7712 | tf_op jit(solution)/shard_map/ppermute | solution.py:236
  89.6 1.7 %collective-permute-start.5 = (f32[3,640]{1,0:T(4,128)S(1)}, f32[3,640]{1,0:T(4,128)S(1)}, u32[]{:S(2)}, u32[]{:S(2)}) collective-permute-start(f32[3,640]{1,0:T(4,128)S(1)} %add.26), channel_id=1, source_target_pairs={{0,128},{64,192},{128,0},{192,64},{1,129},{65,193},{129,1},{193,65... | collective-permute-start | bytes 23048 | tf_op jit(solution)/shard_map/ppermute | solution.py:236
  91.3 2.8 %collective-permute-done.5 = f32[3,640]{1,0:T(4,128)S(1)} collective-permute-done((f32[3,640]{1,0:T(4,128)S(1)}, f32[3,640]{1,0:T(4,128)S(1)}, u32[]{:S(2)}, u32[]{:S(2)}) %collective-permute-start.5) | collective-permute-done | bytes 7712 | tf_op jit(solution)/shard_map/ppermute | solution.py:236
  94.2 0.3 collective-permute-start.6
  94.5 7.3 %collective-permute-done.6 = f32[3,640]{1,0:T(4,128)S(1)} collective-permute-done((f32[3,640]{1,0:T(4,128)S(1)}, f32[3,640]{1,0:T(4,128)S(1)}, u32[]{:S(2)}, u32[]{:S(2)}) %collective-permute-start.6) | collective-permute-done | bytes 7712 | tf_op jit(solution)/shard_map/ppermute | solution.py:236
  101.8 0.0 collective-permute-start.7
  101.8 5.5 %collective-permute-done.7 = f32[3,640]{1,0:T(4,128)S(1)} collective-permute-done((f32[3,640]{1,0:T(4,128)S(1)}, f32[3,640]{1,0:T(4,128)S(1)}, u32[]{:S(2)}, u32[]{:S(2)}) %collective-permute-start.7) | collective-permute-done | bytes 7712 | tf_op jit(solution)/shard_map/ppermute | solution.py:236
  107.2 2.2 %collective-permute-start.8 = (f32[3,640]{1,0:T(4,128)S(1)}, f32[3,640]{1,0:T(4,128)S(1)}, u32[]{:S(2)}, u32[]{:S(2)}) collective-permute-start(f32[3,640]{1,0:T(4,128)S(1)} %add.29), channel_id=1, source_target_pairs={{0,16},{4,20},{8,24},{12,28},{16,0},{20,4},{24,8},{28,12},{32,48},... | collective-permute-start | bytes 23048 | tf_op jit(solution)/shard_map/ppermute | solution.py:236
  109.5 1.6 %collective-permute-done.8 = f32[3,640]{1,0:T(4,128)S(1)} collective-permute-done((f32[3,640]{1,0:T(4,128)S(1)}, f32[3,640]{1,0:T(4,128)S(1)}, u32[]{:S(2)}, u32[]{:S(2)}) %collective-permute-start.8) | collective-permute-done | bytes 7712 | tf_op jit(solution)/shard_map/ppermute | solution.py:236
  111.1 3.8 %collective-permute-start.9 = (f32[3,640]{1,0:T(4,128)S(1)}, f32[3,640]{1,0:T(4,128)S(1)}, u32[]{:S(2)}, u32[]{:S(2)}) collective-permute-start(f32[3,640]{1,0:T(4,128)S(1)} %add.30), channel_id=1, source_target_pairs={{0,32},{4,36},{8,40},{12,44},{16,48},{20,52},{24,56},{28,60},{32,0... | collective-permute-start | bytes 23048 | tf_op jit(solution)/shard_map/ppermute | solution.py:236
  114.9 0.0 all-to-all-done.1.rc_ref
  114.9 5.8 %shard_map.104 = (f32[16,40,640]{2,1,0:T(8,128)}, f32[1,640]{1,0:T(1,128)}) custom-call(s32[16]{0:T(128)} %bitcast.24, bf16[16,2,40,640]{3,2,1,0:T(8,128)(2,1)} %all-to-all-done.1.rc_ref, bf16[16,40,640]{2,1,0:T(8,128)(2,1)} %bitcast.14), custom_call_target="tpu_custom_call" | custom-call | flops 2000000 | bytes 6000000 | tf_op jit(solution)/shard_map/pallas_call | solution.py:301
  120.8 0.0 collective-permute-start.2
  120.8 1.4 collective-permute-done.2
  122.1 0.7 add.25.i1_ref
  122.8 0.0 copy-start.3
  122.8 5.3 %collective-permute-start.3 = (f32[1,640]{1,0:T(1,128)S(1)}, f32[1,640]{1,0:T(1,128)S(1)}, u32[]{:S(2)}, u32[]{:S(2)}) collective-permute-start(f32[1,640]{1,0:T(1,128)S(1)} %add.25.i1_ref), channel_id=1, source_target_pairs={{0,2},{1,3},{2,0},{3,1},{4,6},{5,7},{6,4},{7,5},{8,10},{9,11},{10,... | collective-permute-start | bytes 7688 | tf_op jit(solution)/shard_map/ppermute | solution.py:236
  128.1 0.0 collective-permute-done.9
  128.1 0.6 add.31
  128.7 1.6 %collective-permute-done.3.i2_ref = f32[1,640]{1,0:T(1,128)S(1)} collective-permute-done((f32[1,640]{1,0:T(1,128)S(1)}, f32[1,640]{1,0:T(1,128)S(1)}, u32[]{:S(2)}, u32[]{:S(2)}) %collective-permute-start.3) | collective-permute-done | bytes 2592 | tf_op jit(solution)/shard_map/ppermute | solution.py:236
  130.3 0.0 copy-start.4
  130.3 0.0 copy-done.3
  130.3 0.6 copy-done.4
  130.9 11.5 %shard_map.105 = (bf16[640,640]{1,0:T(8,128)(2,1)}, bf16[640,640]{1,0:T(8,128)(2,1)}, bf16[640,640]{1,0:T(8,128)(2,1)}) custom-call(bf16[640,640]{1,0:T(8,128)(2,1)} %bitcast.16, bf16[640,640]{1,0:T(8,128)(2,1)} %bitcast.18, bf16[640,640]{1,0:T(8,128)(2,1)} %bitcast.20, bf16[5,640,640]{2,1,0:T(8,128)(2,1)} %get-tuple-element.19.p_ref, ...), custom_call_target="tpu_custom_call" | custom-call | flops 9000000 | bytes 27000000 | tf_op jit(solution)/shard_map/pallas_call | solution.py:312
  (5 shorter events, 0.0 us)
Async XLA Ops:
  14.0 1.4 collective-permute-start
  16.1 8.8 %copy-start = (f32[1,640]{1,0:T(1,128)}, f32[1,640]{1,0:T(1,128)S(1)}, u32[]{:S(2)}) copy-start(f32[1,640]{1,0:T(1,128)S(1)} %add.24.one_ref.s1_ref) | copy-start | bytes 7684
  16.1 8.8 %collective-permute-start.1 = (f32[1,640]{1,0:T(1,128)S(1)}, f32[1,640]{1,0:T(1,128)S(1)}, u32[]{:S(2)}, u32[]{:S(2)}) collective-permute-start(f32[1,640]{1,0:T(1,128)S(1)} %add.24.one_ref.s1_ref), channel_id=1, source_target_pairs={{0,2},{1,3},{2,0},{3,1},{4,6},{5,7},{6,4},{7,5},{8,10},{9,11},{10,... | collective-permute-start | bytes 7688 | tf_op jit(solution)/shard_map/ppermute | solution.py:236
  24.9 0.6 copy-start.2
  80.1 5.8 %copy-start.1 = (f32[3,640]{1,0:T(4,128)S(1)}, f32[3,640]{1,0:T(4,128)}, u32[]{:S(2)}) copy-start(f32[3,640]{1,0:T(4,128)} %get-tuple-element.26) | copy-start | bytes 23044
  80.1 34.9 %all-to-all-start.1 = ((bf16[16,2,40,640]{3,2,1,0:T(8,128)(2,1)}), bf16[16,2,40,640]{3,2,1,0:T(8,128)(2,1)}, u32[]{:S(2)}, u32[]{:S(2)}) async-start(bf16[16,2,40,640]{3,2,1,0:T(8,128)(2,1)} %get-tuple-element.20), calls=%async_computation.1 | async-start | bytes 3276800 | tf_op jit(solution)/shard_map/all_to_all | solution.py:245
  85.8 3.8 %collective-permute-start.4 = (f32[3,640]{1,0:T(4,128)S(1)}, f32[3,640]{1,0:T(4,128)S(1)}, u32[]{:S(2)}, u32[]{:S(2)}) collective-permute-start(f32[3,640]{1,0:T(4,128)S(1)} %copy-done.1), channel_id=1, source_target_pairs={{0,64},{64,0},{128,192},{192,128},{1,65},{65,1},{129,193},{193,129... | collective-permute-start | bytes 23048 | tf_op jit(solution)/shard_map/ppermute | solution.py:236
  89.6 4.6 %collective-permute-start.5 = (f32[3,640]{1,0:T(4,128)S(1)}, f32[3,640]{1,0:T(4,128)S(1)}, u32[]{:S(2)}, u32[]{:S(2)}) collective-permute-start(f32[3,640]{1,0:T(4,128)S(1)} %add.26), channel_id=1, source_target_pairs={{0,128},{64,192},{128,0},{192,64},{1,129},{65,193},{129,1},{193,65... | collective-permute-start | bytes 23048 | tf_op jit(solution)/shard_map/ppermute | solution.py:236
  94.2 7.6 %collective-permute-start.6 = (f32[3,640]{1,0:T(4,128)S(1)}, f32[3,640]{1,0:T(4,128)S(1)}, u32[]{:S(2)}, u32[]{:S(2)}) collective-permute-start(f32[3,640]{1,0:T(4,128)S(1)} %add.27), channel_id=1, source_target_pairs={{0,4},{4,0},{8,12},{12,8},{16,20},{20,16},{24,28},{28,24},{32,36},... | collective-permute-start | bytes 23048 | tf_op jit(solution)/shard_map/ppermute | solution.py:236
  101.8 5.5 %collective-permute-start.7 = (f32[3,640]{1,0:T(4,128)S(1)}, f32[3,640]{1,0:T(4,128)S(1)}, u32[]{:S(2)}, u32[]{:S(2)}) collective-permute-start(f32[3,640]{1,0:T(4,128)S(1)} %add.28), channel_id=1, source_target_pairs={{0,8},{4,12},{8,0},{12,4},{16,24},{20,28},{24,16},{28,20},{32,40},... | collective-permute-start | bytes 23048 | tf_op jit(solution)/shard_map/ppermute | solution.py:236
  107.2 3.9 %collective-permute-start.8 = (f32[3,640]{1,0:T(4,128)S(1)}, f32[3,640]{1,0:T(4,128)S(1)}, u32[]{:S(2)}, u32[]{:S(2)}) collective-permute-start(f32[3,640]{1,0:T(4,128)S(1)} %add.29), channel_id=1, source_target_pairs={{0,16},{4,20},{8,24},{12,28},{16,0},{20,4},{24,8},{28,12},{32,48},... | collective-permute-start | bytes 23048 | tf_op jit(solution)/shard_map/ppermute | solution.py:236
  111.1 17.0 %collective-permute-start.9 = (f32[3,640]{1,0:T(4,128)S(1)}, f32[3,640]{1,0:T(4,128)S(1)}, u32[]{:S(2)}, u32[]{:S(2)}) collective-permute-start(f32[3,640]{1,0:T(4,128)S(1)} %add.30), channel_id=1, source_target_pairs={{0,32},{4,36},{8,40},{12,44},{16,48},{20,52},{24,56},{28,60},{32,0... | collective-permute-start | bytes 23048 | tf_op jit(solution)/shard_map/ppermute | solution.py:236
  120.8 1.4 collective-permute-start.2
  122.8 7.5 %copy-start.3 = (f32[1,640]{1,0:T(1,128)}, f32[1,640]{1,0:T(1,128)S(1)}, u32[]{:S(2)}) copy-start(f32[1,640]{1,0:T(1,128)S(1)} %add.25.i1_ref) | copy-start | bytes 7684
  122.8 7.5 %collective-permute-start.3 = (f32[1,640]{1,0:T(1,128)S(1)}, f32[1,640]{1,0:T(1,128)S(1)}, u32[]{:S(2)}, u32[]{:S(2)}) collective-permute-start(f32[1,640]{1,0:T(1,128)S(1)} %add.25.i1_ref), channel_id=1, source_target_pairs={{0,2},{1,3},{2,0},{3,1},{4,6},{5,7},{6,4},{7,5},{8,10},{9,11},{10,... | collective-permute-start | bytes 7688 | tf_op jit(solution)/shard_map/ppermute | solution.py:236
  130.3 0.6 copy-start.4

commit v2 on v1

v2 whole, which is shorter than its diff:
```python
import math

import jax
import jax.numpy as jnp
from jax import lax
from jax.experimental import pallas as pl
from jax.experimental.pallas import tpu as pltpu
from jax.sharding import PartitionSpec as P


HEADS = 20
HD = 128
TILES = 16
TT = 40
TOK = TILES * TT
WIDTH = HEADS * HD
HERE = 5
EPS = 1e-06
SCALE = 1.0 / math.sqrt(HD)
LOG2E = math.log2(math.e)
RB = 320
BLOCKS = TOK // RB
F32 = jnp.float32
BF16 = jnp.bfloat16


def dot_nt(a, b):
    return lax.dot_general(a, b, (((1,), (1,)), ((), ())), preferred_element_type=F32)


def dot_nn(a, b):
    return lax.dot_general(a, b, (((1,), (0,)), ((), ())), preferred_element_type=F32)


def row_sums(x):
    ones = jnp.ones((8, x.shape[1]), F32)
    return lax.dot_general(
        ones, x, (((1,), (1,)), ((), ())), preferred_element_type=F32, precision=lax.Precision.HIGHEST
    )


def column_sum(x):
    x = jnp.sum(x.reshape(10, 64, HD), axis=0)
    return jnp.sum(x, axis=0, keepdims=True)


def as_column(row):
    return jnp.broadcast_to(row, (128, row.shape[1])).T


def softmax_rows(s):
    top = jnp.max(s, axis=-1, keepdims=True)
    e = jnp.exp2((s - top) * (SCALE * LOG2E))
    return (e * (1.0 / jnp.sum(e, axis=-1, keepdims=True))).astype(BF16)


def lanes(h):
    return pl.ds(pl.multiple_of(h * HD, HD), HD)


def spatial_forward(q_hbm, k_hbm, v_hbm, o_ref, p_ref, ss_ref, q_ref, k_ref, v_ref, acc, sems):
    h = pl.program_id(0)

    @pl.when(h == 0)
    def _():
        copies = [
            pltpu.make_async_copy(a, b, sems.at[i])
            for i, (a, b) in enumerate(((k_hbm, k_ref), (q_hbm, q_ref), (v_hbm, v_ref)))
        ]
        for copy in copies:
            copy.start()
        acc[...] = jnp.zeros_like(acc)
        for copy in copies:
            copy.wait()

    k = k_ref[:, lanes(h)]
    vw = jnp.concatenate([v_ref[:, lanes(h)], jnp.ones((TOK, HD), BF16)], axis=1)
    for i in range(BLOCKS):
        rows = slice(i * RB, (i + 1) * RB)
        p = softmax_rows(dot_nt(q_ref[rows, lanes(h)], k))
        p_ref[h, rows, :] = p
        o = dot_nn(p, vw)[:, :HD].astype(BF16)
        o_ref[rows, lanes(h)] = o
        of = o.astype(F32)
        acc[rows, :] += of * of

    @pl.when(h == HERE - 1)
    def _():
        ss_ref[...] = row_sums(acc[...])[0:1]


def pack_normed(warp, sp_ref, one_ref, two_ref, send_ref, n_ref):
    inv = lax.rsqrt((one_ref[...] + two_ref[...]) / WIDTH + EPS)
    inv = as_column(inv)
    for j in range(TILES):
        col = inv[j * TT : (j + 1) * TT]
        normed = (sp_ref[j].astype(F32) * jnp.concatenate([col] * HERE, axis=1)).astype(BF16)
        n_ref[j] = normed
        send_ref[j, :TT] = normed
    for j in range(TILES):
        send_ref[j, TT:] = n_ref[warp[j]]


def temporal(rc_ref, g_ref, gain_ref, out_ref, send_ref, qs, ks, vs, ps, ts, ds, terms):
    h = pl.program_id(0)

    @pl.when(h == 0)
    def _():
        ps[...] = jnp.zeros_like(ps)
        ts[...] = jnp.zeros_like(ts)

    gq, gk, gv = gain_ref[0:1, lanes(h)], gain_ref[1:2, lanes(h)], gain_ref[2:3, lanes(h)]
    normed = rc_ref[:, :TT, lanes(h)].astype(F32).reshape(TOK, HD)
    warped = rc_ref[:, TT:, lanes(h)].astype(F32).reshape(TOK, HD)
    qs[...] = (normed * gq).astype(BF16)
    ks[...] = (warped * gk).astype(BF16)
    vs[...] = (warped * gv).astype(BF16)
    for i in range(BLOCKS):
        rows = slice(i * RB, (i + 1) * RB)
        last = ((i * RB + RB - 1) // TT + 1) * TT
        keys = max(min(-(-last // HD) * HD, TOK), 2 * HD)
        clear = ((i * RB) // TT + 1) * TT // HD * HD
        g = g_ref[rows, lanes(h)]
        k = ks[:keys, :]
        v = vs[:keys, :]
        s = dot_nt(qs[rows, :], k)
        row = lax.broadcasted_iota(jnp.int32, (RB, 1), 0).astype(F32) + (i * RB + 0.5)
        limit = (jnp.floor(row * (1.0 / TT)) + 1.0) * TT
        col = lax.broadcasted_iota(jnp.int32, (RB, keys - clear), 1).astype(F32) + clear
        masked = jnp.where(col < limit, s[:, clear:], -1e30)
        s = jnp.concatenate([s[:, :clear], masked], axis=1) if clear else masked
        p = softmax_rows(s)
        ps[rows, :keys] = p
        o = dot_nn(p, v)
        out_ref[rows, :] = o.astype(BF16)
        inner = jnp.sum(g.astype(F32) * o, axis=-1, keepdims=True)
        t = p * (dot_nt(g, v) - inner).astype(BF16)
        ts[rows, :keys] = t
        ds[rows, :] = dot_nn(t, k) * SCALE

    def by_keys(lt, right):
        parts = [
            dot_nn(lt, right[:, : 2 * HD]),
            dot_nn(lt[:, HD:], right[HD:, 2 * HD : 4 * HD]),
            dot_nn(lt[:, 3 * HD :], right[3 * HD :, 4 * HD :]),
        ]
        return jnp.concatenate([x.T for x in parts], axis=0)

    dk = by_keys(qs[...].T, ts) * SCALE
    dv = by_keys(g_ref[:, lanes(h)].T, ps)
    dq = ds[...]
    normed = rc_ref[:, :TT, lanes(h)].astype(F32).reshape(TOK, HD)
    warped = rc_ref[:, TT:, lanes(h)].astype(F32).reshape(TOK, HD)
    send_ref[:, :TT, lanes(h)] = (dq * gq).reshape(TILES, TT, HD).astype(BF16)
    send_ref[:, TT : 2 * TT, lanes(h)] = (dk * gk + dv * gv).reshape(TILES, TT, HD).astype(BF16)
    terms[0:1, :] = column_sum(dq * normed)
    terms[1:2, :] = column_sum(dk * warped)
    terms[2:3, :] = column_sum(dv * warped)
    high = terms[0:3].astype(BF16).astype(F32)
    low = terms[0:3] - high
    send_ref[:, 2 * TT :, lanes(h)] = jnp.broadcast_to(
        jnp.concatenate([high, low, high[0:2]], axis=0)[None], (TILES, 8, HD)
    ).astype(BF16)


def gather_back(warp, rc_ref, sp_ref, gn_ref, in_ref, terms_ref):
    gn_ref[...] = rc_ref[:, :TT].astype(F32)
    for j in range(TILES):
        gn_ref[warp[j]] += rc_ref[j, TT : 2 * TT].astype(F32)
    total = jnp.sum(rc_ref[:, 2 * TT :].astype(F32), axis=0)
    terms_ref[...] = total[0:3] + total[3:6]
    prod = gn_ref[...] * sp_ref[...].astype(F32)
    prod = prod.reshape(TOK, HERE * HD)
    prod = sum(prod[:, h * HD : (h + 1) * HD] for h in range(HERE))
    in_ref[...] = row_sums(prod)[0:1]


def spatial_backward(
    q_ref, k_ref, v_ref, p_ref, sp_ref, gn_ref, s1_ref, s2_ref, i1_ref, i2_ref,
    dq_ref, dk_ref, dv_ref, inv_s, shift, gb, ts,
):
    h = pl.program_id(0)

    @pl.when(h == 0)
    def _():
        inv = lax.rsqrt((s1_ref[...] + s2_ref[...]) / WIDTH + EPS)
        inv_s[...] = as_column(inv)
        shift[...] = as_column(inv * inv * inv * ((i1_ref[...] + i2_ref[...]) / WIDTH))

    k = k_ref[:, lanes(h)]
    v = v_ref[:, lanes(h)]
    for i in range(BLOCKS):
        rows = slice(i * RB, (i + 1) * RB)
        spatial = sp_ref[rows, lanes(h)].astype(F32)
        grad = inv_s[rows, :] * gn_ref[rows, lanes(h)] - spatial * shift[rows, :]
        g = grad.astype(BF16)
        gb[rows, :] = g
        inner = jnp.sum(g.astype(F32) * spatial, axis=-1, keepdims=True)
        t = p_ref[h, rows, :] * (dot_nt(g, v) - inner).astype(BF16)
        ts[rows, :] = t
        dq_ref[rows, :] = (dot_nn(t, k) * SCALE).astype(BF16)
    dk_ref[...] = (dot_nn(q_ref[:, lanes(h)].T, ts[...]) * SCALE).T.astype(BF16)
    dv_ref[...] = dot_nn(gb[...].T, p_ref[h]).T.astype(BF16)


def columns(rows=TOK):
    return pl.BlockSpec((rows, HD), lambda h, *_: (0, h))


def call(kernel, grid, in_specs, out_specs, out_shape, scratch, us, prefetch=0, limit=24):
    return pl.pallas_call(
        kernel,
        grid_spec=pltpu.PrefetchScalarGridSpec(
            num_scalar_prefetch=prefetch,
            grid=grid,
            in_specs=in_specs,
            out_specs=out_specs,
            scratch_shapes=scratch,
        ),
        out_shape=out_shape,
        cost_estimate=pl.CostEstimate(
            flops=int(us * 1e6), bytes_accessed=int(us * 3.0e6), transcendentals=0
        ),
        compiler_params=pltpu.CompilerParams(vmem_limit_bytes=limit * 1024 * 1024),
    )


def swapped(x, axis, flip):
    size = lax.axis_size(axis)
    return lax.ppermute(x, axis, [(i, i ^ flip) for i in range(size)])


def half_sums(x, axis):
    other = swapped(x, axis, 1)
    x = x + other
    return x, swapped(x, axis, 2)


def exchanged(x):
    return lax.all_to_all(x, "frame", 0, 0, tiled=True)


def body(query_spatial, key_spatial, value_spatial, gains, warp_lists, cotangent):
    width = HERE * HD
    q = query_spatial.reshape(TOK, width)
    k = key_spatial.reshape(TOK, width)
    v = value_spatial.reshape(TOK, width)
    g = cotangent.reshape(TOK, width)
    warp = warp_lists[0, 0]
    sds = jax.ShapeDtypeStruct
    tall = pltpu.VMEM((TOK, HD), F32)
    thin = pltpu.VMEM((TOK, HD), BF16)
    big = pltpu.VMEM((TOK, TOK), BF16)
    held = pl.BlockSpec(memory_space=pltpu.VMEM)
    away = pl.BlockSpec(memory_space=pltpu.HBM)
    line = sds((1, TOK), F32)
    flat = sds((TOK, width), BF16)
    three = sds((3, width), F32)
    heads = (HERE,)

    spatial, probs, squares = call(
        spatial_forward,
        heads,
        [away] * 3,
        [held] * 3,
        [flat, sds((HERE, TOK, TOK), BF16), line],
        [big, big, big, tall, pltpu.SemaphoreType.DMA((3,))],
        7,
    )(*(pltpu.with_memory_space_constraint(x, pltpu.HBM) for x in (q, k, v)))
    ss_one, ss_two = half_sums(squares, "mp")
    spatial_tiles = spatial.reshape(TILES, TT, width)
    send = call(
        pack_normed,
        (),
        [held] * 3,
        held,
        sds((TILES, 2 * TT, width), BF16),
        [pltpu.VMEM((TILES, TT, width), BF16)],
        1,
        prefetch=1,
    )(warp, spatial_tiles, ss_one, ss_two)
    got = exchanged(send)

    out, back = call(
        temporal,
        heads,
        [held] * 3,
        [columns(), held],
        [flat, sds((TILES, 2 * TT + 8, width), BF16)],
        [thin, thin, thin, big, big, tall, pltpu.VMEM((8, HD), F32)],
        16,
    )(got, g, gains)
    came = exchanged(back)

    grad_normed, inner, terms = call(
        gather_back,
        (),
        [held] * 2,
        [held] * 3,
        [sds((TILES, TT, width), F32), line, three],
        [],
        2,
        prefetch=1,
    )(warp, came, spatial_tiles)
    in_one, in_two = half_sums(inner, "mp")
    t_one, t_two = half_sums(terms, "clip")

    dq, dk, dv = call(
        spatial_backward,
        heads,
        [held] * 10,
        [columns()] * 3,
        [flat] * 3,
        [tall, tall, thin, big],
        9,
    )(
        q, k, v, probs, spatial, grad_normed.reshape(TOK, width),
        ss_one, ss_two, in_one, in_two,
    )
    return (
        out.reshape(cotangent.shape),
        dq.reshape(query_spatial.shape),
        dk.reshape(query_spatial.shape),
        dv.reshape(query_spatial.shape),
        t_one + t_two,
    )


def solution(mesh):
    frames = P("clip", "frame", None, None, "mp")
    tiles = P("clip", None, "frame", None, "mp")
    return jax.shard_map(
        body,
        mesh=mesh,
        in_specs=(frames, frames, frames, P(None, "mp"), P("clip", "frame", None), tiles),
        out_specs=(tiles, frames, frames, frames, P(None, "mp")),
        check_vma=False,
    )
```

time: 144 us -> 109 us (0.76)
  Pallas kernels: 56.3 us -> 27 us
  blocking collectives: 29 us -> 55.4 us
  waiting for transfers between devices: 25.8 us -> 8.62 us
  starting transfers between devices: 27.4 us -> 15.4 us
    pallas_call x5, Pallas kernels: 56.3 us -> 27 us  [the longest x1 10.7 us: body(): call(temporal, heads, [held] * 3, [columns(), held], [flat, sds((TILES, 2...]
    all_to_all x1 -> x2, blocking collectives: 29 us -> 55.4 us  [exchanged(): return lax.all_to_all(x, 'frame', 0, 0, tiled=True)]
    ppermute x10 -> x6, waiting for transfers between devices: 25.8 us -> 8.62 us  [swapped(): return lax.ppermute(x, axis, [(i, i ^ flip) for i in range(size)])]
    ppermute x10 -> x6, starting transfers between devices: 21.7 us -> 15.4 us  [swapped(): return lax.ppermute(x, axis, [(i, i ^ flip) for i in range(size)])]
    all_to_all x1 -> x0, starting transfers between devices: 5.76 us -> none  [exchanged(): return lax.all_to_all(x, 'frame', 0, 0, tiled=True)]
  transfers between devices with their start and end apart: 11 -> 6, of which waited for: 9 -> 5; matrix products, arithmetic and copies ran while one was open for 1% -> 0% of each run, Pallas kernels for 4% -> 6%
where the time goes in v2:
time: 109 us; the launch traced here: 108 us
  blocking collectives  55.4 us (51%)
  Pallas kernels  27 us (25%)
  starting transfers between devices  15.4 us (14%)
  waiting for transfers between devices  8.62 us (8%)
    all_to_all x2, blocking collectives, exchanged(): return lax.all_to_all(x, 'frame', 0, 0, tiled=True)  55.4 us
    ppermute x6, starting transfers between devices, swapped(): return lax.ppermute(x, axis, [(i, i ^ flip) for i in range(size)])  15.4 us
    pallas_call x1, Pallas kernels, body(): call(temporal, heads, [held] * 3, [columns(), held], [flat, sds((TILES, 2...  10.7 us
    ppermute x6, waiting for transfers between devices, swapped(): return lax.ppermute(x, axis, [(i, i ^ flip) for i in range(size)])  8.62 us
    pallas_call x1, Pallas kernels, body(): call(spatial_forward, heads, [away] * 3, [held] * 3, [flat, sds((HERE, TO...  7.62 us
    pallas_call x1, Pallas kernels, body(): call(spatial_backward, heads, [held] * 10, [columns()] * 3, [flat] * 3, [...  6.47 us
  transfers between devices with their start and end apart: 6, of which 5 were waited for; matrix products, arithmetic and copies ran while one was open for 0% of the time, Pallas kernels for 6%

profile of v2, /device:TPU:8, one launch (start us, length us, event | category | flops | bytes accessed | tf_op | source)
XLA Modules:
  0.0 107.8 jit_solution(6051303197891631370)
XLA Ops:
  0.6 0.0 copy-start.5
  0.6 7.6 %shard_map.101 = (bf16[640,640]{1,0:T(8,128)(2,1)S(1)}, bf16[5,640,640]{2,1,0:T(8,128)(2,1)S(1)}, f32[1,640]{1,0:T(1,128)S(1)}) custom-call(bf16[640,640]{1,0:T(8,128)(2,1)} %bitcast.15, bf16[640,640]{1,0:T(8,128)(2,1)} %bitcast.17, bf16[640,640]{1,0:T(8,128)(2,1)} %bitcast.19), custom_call_target="tpu_custom_call" | custom-call | flops 7000000 | bytes 21000000 | tf_op jit(solution)/shard_map/pallas_call | solution.py:261
  8.3 0.1 collective-permute-start
  8.4 1.2 %collective-permute-done = f32[1,640]{1,0:T(1,128)S(1)} collective-permute-done((f32[1,640]{1,0:T(1,128)S(1)}, f32[1,640]{1,0:T(1,128)S(1)}, u32[]{:S(2)}, u32[]{:S(2)}) %collective-permute-start) | collective-permute-done | bytes 2592 | tf_op jit(solution)/shard_map/ppermute | solution.py:230
  9.5 7.2 %collective-permute-start.1 = (f32[1,640]{1,0:T(1,128)S(1)}, f32[1,640]{1,0:T(1,128)S(1)}, u32[]{:S(2)}, u32[]{:S(2)}) collective-permute-start(f32[1,640]{1,0:T(1,128)S(1)} %add.12.one_ref.s1_ref), channel_id=1, source_target_pairs={{0,2},{1,3},{2,0},{3,1},{4,6},{5,7},{6,4},{7,5},{8,10},{9,11},{10,... | collective-permute-start | bytes 7688 | tf_op jit(solution)/shard_map/ppermute | solution.py:230
  16.7 1.6 %collective-permute-done.1.two_ref.s2_ref = f32[1,640]{1,0:T(1,128)S(1)} collective-permute-done((f32[1,640]{1,0:T(1,128)S(1)}, f32[1,640]{1,0:T(1,128)S(1)}, u32[]{:S(2)}, u32[]{:S(2)}) %collective-permute-start.1) | collective-permute-done | bytes 2592 | tf_op jit(solution)/shard_map/ppermute | solution.py:230
  18.3 0.0 copy-done.5
  18.3 0.8 shard_map.102
  19.1 0.0 copy-start.3
  19.1 0.0 copy-start.4
  19.1 28.9 %all_to_all.10.rc_ref = bf16[16,80,640]{2,1,0:T(8,128)(2,1)S(1)} all-to-all(bf16[16,80,640]{2,1,0:T(8,128)(2,1)S(1)} %shard_map.102), channel_id=1, replica_groups=mesh['clip'=4,'frame'=16,'mp'=4] {'frame'}, dimensions={0} | all-to-all | bytes 3276800 | tf_op jit(solution)/shard_map/all_to_all | solution.py:240
  48.0 0.0 copy-done.3
  48.0 0.0 copy-done.4
  48.0 10.7 %shard_map.103 = (bf16[640,640]{1,0:T(8,128)(2,1)}, bf16[16,88,640]{2,1,0:T(8,128)(2,1)S(1)}) custom-call(bf16[16,80,640]{2,1,0:T(8,128)(2,1)S(1)} %all_to_all.10.rc_ref, bf16[640,640]{1,0:T(8,128)(2,1)S(1)} %bitcast.22, f32[3,640]{1,0:T(4,128)S(1)} %copy-done.4), custom_call_target="tpu_custom_call" | custom-call | flops 16000000 | bytes 48000000 | tf_op jit(solution)/shard_map/pallas_call | solution.py:284
  58.7 26.6 %all_to_all.11.rc_ref = bf16[16,88,640]{2,1,0:T(8,128)(2,1)S(1)} all-to-all(bf16[16,88,640]{2,1,0:T(8,128)(2,1)S(1)} %get-tuple-element.20), channel_id=1, replica_groups=mesh['clip'=4,'frame'=16,'mp'=4] {'frame'}, dimensions={0} | all-to-all | bytes 3604480 | tf_op jit(solution)/shard_map/all_to_all | solution.py:240
  85.3 0.0 copy-start
  85.3 0.0 copy-start.1
  85.3 0.0 copy-start.2
  85.3 1.3 %shard_map.104 = (f32[16,40,640]{2,1,0:T(8,128)S(1)}, f32[1,640]{1,0:T(1,128)S(1)}, f32[3,640]{1,0:T(4,128)S(1)}) custom-call(s32[16]{0:T(128)S(1)} %bitcast.24, bf16[16,88,640]{2,1,0:T(8,128)(2,1)S(1)} %all_to_all.11.rc_ref, bf16[16,40,640]{2,1,0:T(8,128)(2,1)S(1)} %bitcast.14), custom_call_target="tpu_custom_call" | custom-call | flops 2000000 | bytes 6000000 | tf_op jit(solution)/shard_map/pallas_call | solution.py:295
  86.7 1.1 collective-permute-start.4
  87.7 2.6 %collective-permute-done.4 = f32[3,640]{1,0:T(4,128)S(1)} collective-permute-done((f32[3,640]{1,0:T(4,128)S(1)}, f32[3,640]{1,0:T(4,128)S(1)}, u32[]{:S(2)}, u32[]{:S(2)}) %collective-permute-start.4) | collective-permute-done | bytes 7712 | tf_op jit(solution)/shard_map/ppermute | solution.py:230
  90.4 1.7 %collective-permute-start.5 = (f32[3,640]{1,0:T(4,128)S(1)}, f32[3,640]{1,0:T(4,128)S(1)}, u32[]{:S(2)}, u32[]{:S(2)}) collective-permute-start(f32[3,640]{1,0:T(4,128)S(1)} %add.14), channel_id=1, source_target_pairs={{0,128},{64,192},{128,0},{192,64},{1,129},{65,193},{129,1},{193,65... | collective-permute-start | bytes 23048 | tf_op jit(solution)/shard_map/ppermute | solution.py:230
  92.0 0.0 collective-permute-start.2
  92.0 1.2 %collective-permute-done.2 = f32[1,640]{1,0:T(1,128)S(1)} collective-permute-done((f32[1,640]{1,0:T(1,128)S(1)}, f32[1,640]{1,0:T(1,128)S(1)}, u32[]{:S(2)}, u32[]{:S(2)}) %collective-permute-start.2) | collective-permute-done | bytes 2592 | tf_op jit(solution)/shard_map/ppermute | solution.py:230
  93.2 5.4 %collective-permute-start.3 = (f32[1,640]{1,0:T(1,128)S(1)}, f32[1,640]{1,0:T(1,128)S(1)}, u32[]{:S(2)}, u32[]{:S(2)}) collective-permute-start(f32[1,640]{1,0:T(1,128)S(1)} %add.13.i1_ref), channel_id=1, source_target_pairs={{0,2},{1,3},{2,0},{3,1},{4,6},{5,7},{6,4},{7,5},{8,10},{9,11},{10,... | collective-permute-start | bytes 7688 | tf_op jit(solution)/shard_map/ppermute | solution.py:230
  98.6 2.1 %collective-permute-done.3.i2_ref = f32[1,640]{1,0:T(1,128)S(1)} collective-permute-done((f32[1,640]{1,0:T(1,128)S(1)}, f32[1,640]{1,0:T(1,128)S(1)}, u32[]{:S(2)}, u32[]{:S(2)}) %collective-permute-start.3) | collective-permute-done | bytes 2592 | tf_op jit(solution)/shard_map/ppermute | solution.py:230
  100.7 0.0 copy-done
  100.7 0.0 copy-done.1
  100.7 0.0 copy-done.2
  100.7 6.5 %shard_map.105 = (bf16[640,640]{1,0:T(8,128)(2,1)}, bf16[640,640]{1,0:T(8,128)(2,1)}, bf16[640,640]{1,0:T(8,128)(2,1)}) custom-call(bf16[640,640]{1,0:T(8,128)(2,1)S(1)} %bitcast.16, bf16[640,640]{1,0:T(8,128)(2,1)S(1)} %bitcast.18, bf16[640,640]{1,0:T(8,128)(2,1)S(1)} %bitcast.20, bf16[5,640,640]{2,1,0:T(8,128)(2,1)S(1)} %get-tuple-element.19.p_ref, ...), custom_call_target="tpu_custom_call" | custom-call | flops 9000000 | bytes 27000000 | tf_op jit(solution)/shard_map/pallas_call | solution.py:308
  107.2 0.0 collective-permute-done.5
  107.2 0.6 add.15
  (3 shorter events, 0.0 us)
Async XLA Ops:
  0.6 17.7 %copy-start.5 = (s32[1,1,16]{2,1,0:T(1,128)S(1)}, s32[1,1,16]{2,1,0:T(1,128)}, u32[]{:S(2)}) copy-start(s32[1,1,16]{2,1,0:T(1,128)} %param.10) | copy-start | bytes 196
  8.3 1.3 %collective-permute-start = (f32[1,640]{1,0:T(1,128)S(1)}, f32[1,640]{1,0:T(1,128)S(1)}, u32[]{:S(2)}, u32[]{:S(2)}) collective-permute-start(f32[1,640]{1,0:T(1,128)S(1)} %get-tuple-element.17), channel_id=1, source_target_pairs={{0,1},{1,0},{2,3},{3,2},{4,5},{5,4},{6,7},{7,6},{8,9},{9,8},{10,11... | collective-permute-start | bytes 7688 | tf_op jit(solution)/shard_map/ppermute | solution.py:230
  9.5 8.8 %collective-permute-start.1 = (f32[1,640]{1,0:T(1,128)S(1)}, f32[1,640]{1,0:T(1,128)S(1)}, u32[]{:S(2)}, u32[]{:S(2)}) collective-permute-start(f32[1,640]{1,0:T(1,128)S(1)} %add.12.one_ref.s1_ref), channel_id=1, source_target_pairs={{0,2},{1,3},{2,0},{3,1},{4,6},{5,7},{6,4},{7,5},{8,10},{9,11},{10,... | collective-permute-start | bytes 7688 | tf_op jit(solution)/shard_map/ppermute | solution.py:230
  19.1 28.9 %copy-start.3 = (bf16[1,16,1,40,640]{4,3,2,1,0:T(8,128)(2,1)S(1)}, bf16[1,16,1,40,640]{4,3,2,1,0:T(8,128)(2,1)}, u32[]{:S(2)}) copy-start(bf16[1,16,1,40,640]{4,3,2,1,0:T(8,128)(2,1)} %param.11) | copy-start | bytes 2457604
  19.1 28.9 %copy-start.4 = (f32[3,640]{1,0:T(4,128)S(1)}, f32[3,640]{1,0:T(4,128)}, u32[]{:S(2)}) copy-start(f32[3,640]{1,0:T(4,128)} %gain_ref.1) | copy-start | bytes 23044
  85.3 15.4 %copy-start = (bf16[1,1,16,40,640]{4,3,2,1,0:T(8,128)(2,1)S(1)}, bf16[1,1,16,40,640]{4,3,2,1,0:T(8,128)(2,1)}, u32[]{:S(2)}) copy-start(bf16[1,1,16,40,640]{4,3,2,1,0:T(8,128)(2,1)} %param.6) | copy-start | bytes 2457604
  85.3 15.4 %copy-start.1 = (bf16[1,1,16,40,640]{4,3,2,1,0:T(8,128)(2,1)S(1)}, bf16[1,1,16,40,640]{4,3,2,1,0:T(8,128)(2,1)}, u32[]{:S(2)}) copy-start(bf16[1,1,16,40,640]{4,3,2,1,0:T(8,128)(2,1)} %param.7) | copy-start | bytes 2457604
  85.3 15.4 %copy-start.2 = (bf16[1,1,16,40,640]{4,3,2,1,0:T(8,128)(2,1)S(1)}, bf16[1,1,16,40,640]{4,3,2,1,0:T(8,128)(2,1)}, u32[]{:S(2)}) copy-start(bf16[1,1,16,40,640]{4,3,2,1,0:T(8,128)(2,1)} %param.8) | copy-start | bytes 2457604
  86.7 3.7 %collective-permute-start.4 = (f32[3,640]{1,0:T(4,128)S(1)}, f32[3,640]{1,0:T(4,128)S(1)}, u32[]{:S(2)}, u32[]{:S(2)}) collective-permute-start(f32[3,640]{1,0:T(4,128)S(1)} %get-tuple-element.26), channel_id=1, source_target_pairs={{0,64},{64,0},{128,192},{192,128},{1,65},{65,1},{129,193},{193,129... | collective-permute-start | bytes 23048 | tf_op jit(solution)/shard_map/ppermute | solution.py:230
  90.4 16.8 %collective-permute-start.5 = (f32[3,640]{1,0:T(4,128)S(1)}, f32[3,640]{1,0:T(4,128)S(1)}, u32[]{:S(2)}, u32[]{:S(2)}) collective-permute-start(f32[3,640]{1,0:T(4,128)S(1)} %add.14), channel_id=1, source_target_pairs={{0,128},{64,192},{128,0},{192,64},{1,129},{65,193},{129,1},{193,65... | collective-permute-start | bytes 23048 | tf_op jit(solution)/shard_map/ppermute | solution.py:230
  92.0 1.2 %collective-permute-start.2 = (f32[1,640]{1,0:T(1,128)S(1)}, f32[1,640]{1,0:T(1,128)S(1)}, u32[]{:S(2)}, u32[]{:S(2)}) collective-permute-start(f32[1,640]{1,0:T(1,128)S(1)} %get-tuple-element.22), channel_id=1, source_target_pairs={{0,1},{1,0},{2,3},{3,2},{4,5},{5,4},{6,7},{7,6},{8,9},{9,8},{10,11... | collective-permute-start | bytes 7688 | tf_op jit(solution)/shard_map/ppermute | solution.py:230
  93.2 7.5 %collective-permute-start.3 = (f32[1,640]{1,0:T(1,128)S(1)}, f32[1,640]{1,0:T(1,128)S(1)}, u32[]{:S(2)}, u32[]{:S(2)}) collective-permute-start(f32[1,640]{1,0:T(1,128)S(1)} %add.13.i1_ref), channel_id=1, source_target_pairs={{0,2},{1,3},{2,0},{3,1},{4,6},{5,7},{6,4},{7,5},{8,10},{9,11},{10,... | collective-permute-start | bytes 7688 | tf_op jit(solution)/shard_map/ppermute | solution.py:230

commit v3 on v2

--- a/solution.py
+++ b/solution.py
@@ -19,6 +19,7 @@
 SCALE = 1.0 / math.sqrt(HD)
 LOG2E = math.log2(math.e)
 RB = 320
+SUB = 160
 BLOCKS = TOK // RB
 F32 = jnp.float32
 BF16 = jnp.bfloat16
@@ -61,17 +62,21 @@
 def spatial_forward(q_hbm, k_hbm, v_hbm, o_ref, p_ref, ss_ref, q_ref, k_ref, v_ref, acc, sems):
     h = pl.program_id(0)
 
+    def copies(n):
+        return [
+            pltpu.make_async_copy(a.at[:, lanes(n)], b.at[:, lanes(n)], sems.at[i, n])
+            for i, (a, b) in enumerate(((k_hbm, k_ref), (q_hbm, q_ref), (v_hbm, v_ref)))
+        ]
+
     @pl.when(h == 0)
     def _():
-        copies = [
-            pltpu.make_async_copy(a, b, sems.at[i])
-            for i, (a, b) in enumerate(((k_hbm, k_ref), (q_hbm, q_ref), (v_hbm, v_ref)))
-        ]
-        for copy in copies:
-            copy.start()
+        for n in range(HERE):
+            for copy in copies(n):
+                copy.start()
         acc[...] = jnp.zeros_like(acc)
-        for copy in copies:
-            copy.wait()
+
+    for copy in copies(h):
+        copy.wait()
 
     k = k_ref[:, lanes(h)]
     vw = jnp.concatenate([v_ref[:, lanes(h)], jnp.ones((TOK, HD), BF16)], axis=1)
@@ -115,28 +120,31 @@
     qs[...] = (normed * gq).astype(BF16)
     ks[...] = (warped * gk).astype(BF16)
     vs[...] = (warped * gv).astype(BF16)
-    for i in range(BLOCKS):
-        rows = slice(i * RB, (i + 1) * RB)
-        last = ((i * RB + RB - 1) // TT + 1) * TT
-        keys = max(min(-(-last // HD) * HD, TOK), 2 * HD)
-        clear = ((i * RB) // TT + 1) * TT // HD * HD
-        g = g_ref[rows, lanes(h)]
-        k = ks[:keys, :]
-        v = vs[:keys, :]
-        s = dot_nt(qs[rows, :], k)
-        row = lax.broadcasted_iota(jnp.int32, (RB, 1), 0).astype(F32) + (i * RB + 0.5)
+    s = dot_nt(qs[...], ks[...])
+    spans = []
+    for i in range(0, TOK, SUB):
+        rows = slice(i, i + SUB)
+        last = ((i + SUB - 1) // TT + 1) * TT
+        keys = min(-(-last // HD) * HD, TOK)
+        clear = (i // TT + 1) * TT // HD * HD
+        spans.append((rows, keys))
+        row = lax.broadcasted_iota(jnp.int32, (SUB, 1), 0).astype(F32) + (i + 0.5)
         limit = (jnp.floor(row * (1.0 / TT)) + 1.0) * TT
-        col = lax.broadcasted_iota(jnp.int32, (RB, keys - clear), 1).astype(F32) + clear
-        masked = jnp.where(col < limit, s[:, clear:], -1e30)
-        s = jnp.concatenate([s[:, :clear], masked], axis=1) if clear else masked
-        p = softmax_rows(s)
-        ps[rows, :keys] = p
-        o = dot_nn(p, v)
-        out_ref[rows, :] = o.astype(BF16)
-        inner = jnp.sum(g.astype(F32) * o, axis=-1, keepdims=True)
-        t = p * (dot_nt(g, v) - inner).astype(BF16)
-        ts[rows, :keys] = t
-        ds[rows, :] = dot_nn(t, k) * SCALE
+        if clear < keys:
+            col = lax.broadcasted_iota(jnp.int32, (SUB, keys - clear), 1).astype(F32) + clear
+            part = jnp.where(col < limit, s[rows, clear:keys], -1e30)
+            part = jnp.concatenate([s[rows, :clear], part], axis=1) if clear else part
+        else:
+            part = s[rows, :keys]
+        ps[rows, :keys] = softmax_rows(part)
+    o = dot_nn(ps[...], vs[...])
+    out_ref[...] = o.astype(BF16)
+    g = g_ref[:, lanes(h)]
+    inner = jnp.sum(g.astype(F32) * o, axis=-1, keepdims=True)
+    dp = dot_nt(g, vs[...])
+    for rows, keys in spans:
+        ts[rows, :keys] = ps[rows, :keys] * (dp[rows, :keys] - inner[rows]).astype(BF16)
+    ds[...] = dot_nn(ts[...], ks[...]) * SCALE
 
     def by_keys(lt, right):
         parts = [
@@ -264,7 +272,7 @@
         [away] * 3,
         [held] * 3,
         [flat, sds((HERE, TOK, TOK), BF16), line],
-        [big, big, big, tall, pltpu.SemaphoreType.DMA((3,))],
+        [big, big, big, tall, pltpu.SemaphoreType.DMA((3, HERE))],
         7,
     )(*(pltpu.with_memory_space_constraint(x, pltpu.HBM) for x in (q, k, v)))
     ss_one, ss_two = half_sums(squares, "mp")

time: 109 us -> 107 us (0.982)
  Pallas kernels: 27 us -> 24.6 us
    pallas_call x1, Pallas kernels: 10.7 us -> 8.84 us  [body(): call(temporal, heads, [held] * 3, [columns(), held], [flat, sds((TILES, 2...]
where the time goes in v3:
time: 107 us; the launch traced here: 105 us
  blocking collectives  55.5 us (52%)
  Pallas kernels  24.6 us (23%)
  starting transfers between devices  15.4 us (14%)
  waiting for transfers between devices  8.65 us (8%)
    all_to_all x2, blocking collectives, exchanged(): return lax.all_to_all(x, 'frame', 0, 0, tiled=True)  55.5 us
    ppermute x6, starting transfers between devices, swapped(): return lax.ppermute(x, axis, [(i, i ^ flip) for i in range(size)])  15.4 us
    pallas_call x1, Pallas kernels, body(): call(temporal, heads, [held] * 3, [columns(), held], [flat, sds((TILES, 2...  8.84 us
    ppermute x6, waiting for transfers between devices, swapped(): return lax.ppermute(x, axis, [(i, i ^ flip) for i in range(size)])  8.65 us
    pallas_call x1, Pallas kernels, body(): call(spatial_forward, heads, [away] * 3, [held] * 3, [flat, sds((HERE, TO...  7.15 us
    pallas_call x1, Pallas kernels, body(): call(spatial_backward, heads, [held] * 10, [columns()] * 3, [flat] * 3, [...  6.47 us
  transfers between devices with their start and end apart: 6, of which 5 were waited for; matrix products, arithmetic and copies ran while one was open for 0% of the time, Pallas kernels for 6%

profile of v3, /device:TPU:8, one launch (start us, length us, event | category | flops | bytes accessed | tf_op | source)
XLA Modules:
  0.0 105.5 jit_solution(18128643238011528309)
XLA Ops:
  0.6 0.0 copy-start.5
  0.6 7.2 %shard_map.101 = (bf16[640,640]{1,0:T(8,128)(2,1)S(1)}, bf16[5,640,640]{2,1,0:T(8,128)(2,1)S(1)}, f32[1,640]{1,0:T(1,128)S(1)}) custom-call(bf16[640,640]{1,0:T(8,128)(2,1)} %bitcast.15, bf16[640,640]{1,0:T(8,128)(2,1)} %bitcast.17, bf16[640,640]{1,0:T(8,128)(2,1)} %bitcast.19), custom_call_target="tpu_custom_call" | custom-call | flops 7000000 | bytes 21000000 | tf_op jit(solution)/shard_map/pallas_call | solution.py:269
  7.8 0.1 collective-permute-start
  7.9 1.2 %collective-permute-done = f32[1,640]{1,0:T(1,128)S(1)} collective-permute-done((f32[1,640]{1,0:T(1,128)S(1)}, f32[1,640]{1,0:T(1,128)S(1)}, u32[]{:S(2)}, u32[]{:S(2)}) %collective-permute-start) | collective-permute-done | bytes 2592 | tf_op jit(solution)/shard_map/ppermute | solution.py:238
  9.1 7.2 %collective-permute-start.1 = (f32[1,640]{1,0:T(1,128)S(1)}, f32[1,640]{1,0:T(1,128)S(1)}, u32[]{:S(2)}, u32[]{:S(2)}) collective-permute-start(f32[1,640]{1,0:T(1,128)S(1)} %add.12.one_ref.s1_ref), channel_id=1, source_target_pairs={{0,2},{1,3},{2,0},{3,1},{4,6},{5,7},{6,4},{7,5},{8,10},{9,11},{10,... | collective-permute-start | bytes 7688 | tf_op jit(solution)/shard_map/ppermute | solution.py:238
  16.2 1.6 %collective-permute-done.1.two_ref.s2_ref = f32[1,640]{1,0:T(1,128)S(1)} collective-permute-done((f32[1,640]{1,0:T(1,128)S(1)}, f32[1,640]{1,0:T(1,128)S(1)}, u32[]{:S(2)}, u32[]{:S(2)}) %collective-permute-start.1) | collective-permute-done | bytes 2592 | tf_op jit(solution)/shard_map/ppermute | solution.py:238
  17.8 0.0 copy-done.5
  17.8 0.8 shard_map.102
  18.6 0.0 copy-start.3
  18.7 0.0 copy-start.4
  18.7 28.9 %all_to_all.10.rc_ref = bf16[16,80,640]{2,1,0:T(8,128)(2,1)S(1)} all-to-all(bf16[16,80,640]{2,1,0:T(8,128)(2,1)S(1)} %shard_map.102), channel_id=1, replica_groups=mesh['clip'=4,'frame'=16,'mp'=4] {'frame'}, dimensions={0} | all-to-all | bytes 3276800 | tf_op jit(solution)/shard_map/all_to_all | solution.py:248
  47.6 0.0 copy-done.3
  47.6 0.0 copy-done.4
  47.6 8.8 %shard_map.103 = (bf16[640,640]{1,0:T(8,128)(2,1)}, bf16[16,88,640]{2,1,0:T(8,128)(2,1)S(1)}) custom-call(bf16[16,80,640]{2,1,0:T(8,128)(2,1)S(1)} %all_to_all.10.rc_ref, bf16[640,640]{1,0:T(8,128)(2,1)S(1)} %bitcast.22, f32[3,640]{1,0:T(4,128)S(1)} %copy-done.4), custom_call_target="tpu_custom_call" | custom-call | flops 16000000 | bytes 48000000 | tf_op jit(solution)/shard_map/pallas_call | solution.py:292
  56.4 26.6 %all_to_all.11.rc_ref = bf16[16,88,640]{2,1,0:T(8,128)(2,1)S(1)} all-to-all(bf16[16,88,640]{2,1,0:T(8,128)(2,1)S(1)} %get-tuple-element.20), channel_id=1, replica_groups=mesh['clip'=4,'frame'=16,'mp'=4] {'frame'}, dimensions={0} | all-to-all | bytes 3604480 | tf_op jit(solution)/shard_map/all_to_all | solution.py:248
  83.0 0.0 copy-start
  83.0 0.0 copy-start.1
  83.0 0.0 copy-start.2
  83.0 1.3 %shard_map.104 = (f32[16,40,640]{2,1,0:T(8,128)S(1)}, f32[1,640]{1,0:T(1,128)S(1)}, f32[3,640]{1,0:T(4,128)S(1)}) custom-call(s32[16]{0:T(128)S(1)} %bitcast.24, bf16[16,88,640]{2,1,0:T(8,128)(2,1)S(1)} %all_to_all.11.rc_ref, bf16[16,40,640]{2,1,0:T(8,128)(2,1)S(1)} %bitcast.14), custom_call_target="tpu_custom_call" | custom-call | flops 2000000 | bytes 6000000 | tf_op jit(solution)/shard_map/pallas_call | solution.py:303
  84.3 1.0 collective-permute-start.4
  85.4 2.7 %collective-permute-done.4 = f32[3,640]{1,0:T(4,128)S(1)} collective-permute-done((f32[3,640]{1,0:T(4,128)S(1)}, f32[3,640]{1,0:T(4,128)S(1)}, u32[]{:S(2)}, u32[]{:S(2)}) %collective-permute-start.4) | collective-permute-done | bytes 7712 | tf_op jit(solution)/shard_map/ppermute | solution.py:238
  88.0 1.7 %collective-permute-start.5 = (f32[3,640]{1,0:T(4,128)S(1)}, f32[3,640]{1,0:T(4,128)S(1)}, u32[]{:S(2)}, u32[]{:S(2)}) collective-permute-start(f32[3,640]{1,0:T(4,128)S(1)} %add.14), channel_id=1, source_target_pairs={{0,128},{64,192},{128,0},{192,64},{1,129},{65,193},{129,1},{193,65... | collective-permute-start | bytes 23048 | tf_op jit(solution)/shard_map/ppermute | solution.py:238
  89.7 0.0 collective-permute-start.2
  89.7 1.2 %collective-permute-done.2 = f32[1,640]{1,0:T(1,128)S(1)} collective-permute-done((f32[1,640]{1,0:T(1,128)S(1)}, f32[1,640]{1,0:T(1,128)S(1)}, u32[]{:S(2)}, u32[]{:S(2)}) %collective-permute-start.2) | collective-permute-done | bytes 2592 | tf_op jit(solution)/shard_map/ppermute | solution.py:238
  90.9 5.4 %collective-permute-start.3 = (f32[1,640]{1,0:T(1,128)S(1)}, f32[1,640]{1,0:T(1,128)S(1)}, u32[]{:S(2)}, u32[]{:S(2)}) collective-permute-start(f32[1,640]{1,0:T(1,128)S(1)} %add.13.i1_ref), channel_id=1, source_target_pairs={{0,2},{1,3},{2,0},{3,1},{4,6},{5,7},{6,4},{7,5},{8,10},{9,11},{10,... | collective-permute-start | bytes 7688 | tf_op jit(solution)/shard_map/ppermute | solution.py:238
  96.3 2.1 %collective-permute-done.3.i2_ref = f32[1,640]{1,0:T(1,128)S(1)} collective-permute-done((f32[1,640]{1,0:T(1,128)S(1)}, f32[1,640]{1,0:T(1,128)S(1)}, u32[]{:S(2)}, u32[]{:S(2)}) %collective-permute-start.3) | collective-permute-done | bytes 2592 | tf_op jit(solution)/shard_map/ppermute | solution.py:238
  98.4 0.0 copy-done
  98.4 0.0 copy-done.1
  98.4 0.0 copy-done.2
  98.4 6.5 %shard_map.105 = (bf16[640,640]{1,0:T(8,128)(2,1)}, bf16[640,640]{1,0:T(8,128)(2,1)}, bf16[640,640]{1,0:T(8,128)(2,1)}) custom-call(bf16[640,640]{1,0:T(8,128)(2,1)S(1)} %bitcast.16, bf16[640,640]{1,0:T(8,128)(2,1)S(1)} %bitcast.18, bf16[640,640]{1,0:T(8,128)(2,1)S(1)} %bitcast.20, bf16[5,640,640]{2,1,0:T(8,128)(2,1)S(1)} %get-tuple-element.19.p_ref, ...), custom_call_target="tpu_custom_call" | custom-call | flops 9000000 | bytes 27000000 | tf_op jit(solution)/shard_map/pallas_call | solution.py:316
  104.9 0.0 collective-permute-done.5
  104.9 0.6 add.15
  (3 shorter events, 0.0 us)
Async XLA Ops:
  0.6 17.2 %copy-start.5 = (s32[1,1,16]{2,1,0:T(1,128)S(1)}, s32[1,1,16]{2,1,0:T(1,128)}, u32[]{:S(2)}) copy-start(s32[1,1,16]{2,1,0:T(1,128)} %param.10) | copy-start | bytes 196
  7.8 1.3 %collective-permute-start = (f32[1,640]{1,0:T(1,128)S(1)}, f32[1,640]{1,0:T(1,128)S(1)}, u32[]{:S(2)}, u32[]{:S(2)}) collective-permute-start(f32[1,640]{1,0:T(1,128)S(1)} %get-tuple-element.17), channel_id=1, source_target_pairs={{0,1},{1,0},{2,3},{3,2},{4,5},{5,4},{6,7},{7,6},{8,9},{9,8},{10,11... | collective-permute-start | bytes 7688 | tf_op jit(solution)/shard_map/ppermute | solution.py:238
  9.1 8.8 %collective-permute-start.1 = (f32[1,640]{1,0:T(1,128)S(1)}, f32[1,640]{1,0:T(1,128)S(1)}, u32[]{:S(2)}, u32[]{:S(2)}) collective-permute-start(f32[1,640]{1,0:T(1,128)S(1)} %add.12.one_ref.s1_ref), channel_id=1, source_target_pairs={{0,2},{1,3},{2,0},{3,1},{4,6},{5,7},{6,4},{7,5},{8,10},{9,11},{10,... | collective-permute-start | bytes 7688 | tf_op jit(solution)/shard_map/ppermute | solution.py:238
  18.6 28.9 %copy-start.3 = (bf16[1,16,1,40,640]{4,3,2,1,0:T(8,128)(2,1)S(1)}, bf16[1,16,1,40,640]{4,3,2,1,0:T(8,128)(2,1)}, u32[]{:S(2)}) copy-start(bf16[1,16,1,40,640]{4,3,2,1,0:T(8,128)(2,1)} %param.11) | copy-start | bytes 2457604
  18.7 28.9 %copy-start.4 = (f32[3,640]{1,0:T(4,128)S(1)}, f32[3,640]{1,0:T(4,128)}, u32[]{:S(2)}) copy-start(f32[3,640]{1,0:T(4,128)} %gain_ref.1) | copy-start | bytes 23044
  83.0 15.4 %copy-start = (bf16[1,1,16,40,640]{4,3,2,1,0:T(8,128)(2,1)S(1)}, bf16[1,1,16,40,640]{4,3,2,1,0:T(8,128)(2,1)}, u32[]{:S(2)}) copy-start(bf16[1,1,16,40,640]{4,3,2,1,0:T(8,128)(2,1)} %param.6) | copy-start | bytes 2457604
  83.0 15.4 %copy-start.1 = (bf16[1,1,16,40,640]{4,3,2,1,0:T(8,128)(2,1)S(1)}, bf16[1,1,16,40,640]{4,3,2,1,0:T(8,128)(2,1)}, u32[]{:S(2)}) copy-start(bf16[1,1,16,40,640]{4,3,2,1,0:T(8,128)(2,1)} %param.7) | copy-start | bytes 2457604
  83.0 15.4 %copy-start.2 = (bf16[1,1,16,40,640]{4,3,2,1,0:T(8,128)(2,1)S(1)}, bf16[1,1,16,40,640]{4,3,2,1,0:T(8,128)(2,1)}, u32[]{:S(2)}) copy-start(bf16[1,1,16,40,640]{4,3,2,1,0:T(8,128)(2,1)} %param.8) | copy-start | bytes 2457604
  84.3 3.7 %collective-permute-start.4 = (f32[3,640]{1,0:T(4,128)S(1)}, f32[3,640]{1,0:T(4,128)S(1)}, u32[]{:S(2)}, u32[]{:S(2)}) collective-permute-start(f32[3,640]{1,0:T(4,128)S(1)} %get-tuple-element.26), channel_id=1, source_target_pairs={{0,64},{64,0},{128,192},{192,128},{1,65},{65,1},{129,193},{193,129... | collective-permute-start | bytes 23048 | tf_op jit(solution)/shard_map/ppermute | solution.py:238
  88.0 16.8 %collective-permute-start.5 = (f32[3,640]{1,0:T(4,128)S(1)}, f32[3,640]{1,0:T(4,128)S(1)}, u32[]{:S(2)}, u32[]{:S(2)}) collective-permute-start(f32[3,640]{1,0:T(4,128)S(1)} %add.14), channel_id=1, source_target_pairs={{0,128},{64,192},{128,0},{192,64},{1,129},{65,193},{129,1},{193,65... | collective-permute-start | bytes 23048 | tf_op jit(solution)/shard_map/ppermute | solution.py:238
  89.7 1.2 %collective-permute-start.2 = (f32[1,640]{1,0:T(1,128)S(1)}, f32[1,640]{1,0:T(1,128)S(1)}, u32[]{:S(2)}, u32[]{:S(2)}) collective-permute-start(f32[1,640]{1,0:T(1,128)S(1)} %get-tuple-element.22), channel_id=1, source_target_pairs={{0,1},{1,0},{2,3},{3,2},{4,5},{5,4},{6,7},{7,6},{8,9},{9,8},{10,11... | collective-permute-start | bytes 7688 | tf_op jit(solution)/shard_map/ppermute | solution.py:238
  90.9 7.5 %collective-permute-start.3 = (f32[1,640]{1,0:T(1,128)S(1)}, f32[1,640]{1,0:T(1,128)S(1)}, u32[]{:S(2)}, u32[]{:S(2)}) collective-permute-start(f32[1,640]{1,0:T(1,128)S(1)} %add.13.i1_ref), channel_id=1, source_target_pairs={{0,2},{1,3},{2,0},{3,1},{4,6},{5,7},{6,4},{7,5},{8,10},{9,11},{10,... | collective-permute-start | bytes 7688 | tf_op jit(solution)/shard_map/ppermute | solution.py:238

commit v4 on v3

--- a/solution.py
+++ b/solution.py
@@ -159,28 +159,36 @@
     dq = ds[...]
     normed = rc_ref[:, :TT, lanes(h)].astype(F32).reshape(TOK, HD)
     warped = rc_ref[:, TT:, lanes(h)].astype(F32).reshape(TOK, HD)
-    send_ref[:, :TT, lanes(h)] = (dq * gq).reshape(TILES, TT, HD).astype(BF16)
-    send_ref[:, TT : 2 * TT, lanes(h)] = (dk * gk + dv * gv).reshape(TILES, TT, HD).astype(BF16)
-    terms[0:1, :] = column_sum(dq * normed)
-    terms[1:2, :] = column_sum(dk * warped)
-    terms[2:3, :] = column_sum(dv * warped)
-    high = terms[0:3].astype(BF16).astype(F32)
-    low = terms[0:3] - high
-    send_ref[:, 2 * TT :, lanes(h)] = jnp.broadcast_to(
-        jnp.concatenate([high, low, high[0:2]], axis=0)[None], (TILES, 8, HD)
-    ).astype(BF16)
+    start = pl.multiple_of(h * 2 * TT, 16)
+    send_ref[:, pl.ds(start, TT), :] = (dq * gq).reshape(TILES, TT, HD).astype(BF16)
+    start = pl.multiple_of(start + TT, 8)
+    send_ref[:, pl.ds(start, TT), :] = (dk * gk + dv * gv).reshape(TILES, TT, HD).astype(BF16)
+    terms[0:1, lanes(h)] = column_sum(dq * normed)
+    terms[1:2, lanes(h)] = column_sum(dk * warped)
+    terms[2:3, lanes(h)] = column_sum(dv * warped)
+
+    @pl.when(h == HERE - 1)
+    def _():
+        blocks = [terms[n // HERE : n // HERE + 1, n % HERE * HD : n % HERE * HD + HD] for n in range(3 * HERE)]
+        stack = jnp.concatenate(blocks + [blocks[0]], axis=0)
+        send_ref[:, HERE * 2 * TT :, :] = jnp.broadcast_to(stack[None], (TILES, 16, HD)).astype(BF16)
 
 
 def gather_back(warp, rc_ref, sp_ref, gn_ref, in_ref, terms_ref):
-    gn_ref[...] = rc_ref[:, :TT].astype(F32)
-    for j in range(TILES):
-        gn_ref[warp[j]] += rc_ref[j, TT : 2 * TT].astype(F32)
-    total = jnp.sum(rc_ref[:, 2 * TT :].astype(F32), axis=0)
-    terms_ref[...] = total[0:3] + total[3:6]
-    prod = gn_ref[...] * sp_ref[...].astype(F32)
-    prod = prod.reshape(TOK, HERE * HD)
-    prod = sum(prod[:, h * HD : (h + 1) * HD] for h in range(HERE))
-    in_ref[...] = row_sums(prod)[0:1]
+    total = jnp.sum(rc_ref[:, HERE * 2 * TT :].astype(F32), axis=0)
+    for n in range(3 * HERE):
+        at = n % HERE * HD
+        terms_ref[n // HERE : n // HERE + 1, at : at + HD] = total[n : n + 1]
+    inner = jnp.zeros((TOK, HD), F32)
+    for h in range(HERE):
+        cols = slice(h * HD, (h + 1) * HD)
+        first = h * 2 * TT
+        gn_ref[:, :, cols] = rc_ref[:, first : first + TT].astype(F32)
+        for j in range(TILES):
+            gn_ref[warp[j], :, cols] += rc_ref[j, first + TT : first + 2 * TT].astype(F32)
+        prod = gn_ref[:, :, cols] * sp_ref[:, :, cols].astype(F32)
+        inner += prod.reshape(TOK, HD)
+    in_ref[...] = row_sums(inner)[0:1]
 
 
 def spatial_backward(
@@ -294,8 +302,8 @@
         heads,
         [held] * 3,
         [columns(), held],
-        [flat, sds((TILES, 2 * TT + 8, width), BF16)],
-        [thin, thin, thin, big, big, tall, pltpu.VMEM((8, HD), F32)],
+        [flat, sds((TILES, HERE * 2 * TT + 16, HD), BF16)],
+        [thin, thin, thin, big, big, tall, pltpu.VMEM((8, width), F32)],
         16,
     )(got, g, gains)
     came = exchanged(back)

time: 107 us -> 107 us (level)
  no operation moved by 1% of the time
where the time goes in v4:
time: 107 us; the launch traced here: 105 us
  blocking collectives  54.6 us (51%)
  Pallas kernels  25.4 us (24%)
  starting transfers between devices  15.3 us (14%)
  waiting for transfers between devices  8.63 us (8%)
    all_to_all x2, blocking collectives, exchanged(): return lax.all_to_all(x, 'frame', 0, 0, tiled=True)  54.6 us
    ppermute x6, starting transfers between devices, swapped(): return lax.ppermute(x, axis, [(i, i ^ flip) for i in range(size)])  15.3 us
    pallas_call x1, Pallas kernels, body(): call(temporal, heads, [held] * 3, [columns(), held], [flat, sds((TILES, H...  9.43 us
    ppermute x6, waiting for transfers between devices, swapped(): return lax.ppermute(x, axis, [(i, i ^ flip) for i in range(size)])  8.63 us
    pallas_call x1, Pallas kernels, body(): call(spatial_forward, heads, [away] * 3, [held] * 3, [flat, sds((HERE, TO...  7.15 us
    pallas_call x1, Pallas kernels, body(): call(spatial_backward, heads, [held] * 10, [columns()] * 3, [flat] * 3, [...  6.47 us
  transfers between devices with their start and end apart: 6, of which 5 were waited for; matrix products, arithmetic and copies ran while one was open for 0% of the time, Pallas kernels for 6%

profile of v4, /device:TPU:8, one launch (start us, length us, event | category | flops | bytes accessed | tf_op | source)
XLA Modules:
  0.0 105.2 jit_solution(10688736203939404765)
XLA Ops:
  0.6 0.0 copy-start.5
  0.6 7.2 %shard_map.101 = (bf16[640,640]{1,0:T(8,128)(2,1)S(1)}, bf16[5,640,640]{2,1,0:T(8,128)(2,1)S(1)}, f32[1,640]{1,0:T(1,128)S(1)}) custom-call(bf16[640,640]{1,0:T(8,128)(2,1)} %bitcast.15, bf16[640,640]{1,0:T(8,128)(2,1)} %bitcast.17, bf16[640,640]{1,0:T(8,128)(2,1)} %bitcast.19), custom_call_target="tpu_custom_call" | custom-call | flops 7000000 | bytes 21000000 | tf_op jit(solution)/shard_map/pallas_call | solution.py:277
  7.8 0.1 collective-permute-start
  7.9 1.2 %collective-permute-done = f32[1,640]{1,0:T(1,128)S(1)} collective-permute-done((f32[1,640]{1,0:T(1,128)S(1)}, f32[1,640]{1,0:T(1,128)S(1)}, u32[]{:S(2)}, u32[]{:S(2)}) %collective-permute-start) | collective-permute-done | bytes 2592 | tf_op jit(solution)/shard_map/ppermute | solution.py:246
  9.1 7.2 %collective-permute-start.1 = (f32[1,640]{1,0:T(1,128)S(1)}, f32[1,640]{1,0:T(1,128)S(1)}, u32[]{:S(2)}, u32[]{:S(2)}) collective-permute-start(f32[1,640]{1,0:T(1,128)S(1)} %add.12.one_ref.s1_ref), channel_id=1, source_target_pairs={{0,2},{1,3},{2,0},{3,1},{4,6},{5,7},{6,4},{7,5},{8,10},{9,11},{10,... | collective-permute-start | bytes 7688 | tf_op jit(solution)/shard_map/ppermute | solution.py:246
  16.2 1.6 %collective-permute-done.1.two_ref.s2_ref = f32[1,640]{1,0:T(1,128)S(1)} collective-permute-done((f32[1,640]{1,0:T(1,128)S(1)}, f32[1,640]{1,0:T(1,128)S(1)}, u32[]{:S(2)}, u32[]{:S(2)}) %collective-permute-start.1) | collective-permute-done | bytes 2592 | tf_op jit(solution)/shard_map/ppermute | solution.py:246
  17.8 0.0 copy-done.5
  17.8 0.8 shard_map.102
  18.6 0.0 copy-start.3
  18.7 0.0 copy-start.4
  18.7 28.9 %all_to_all.10.rc_ref = bf16[16,80,640]{2,1,0:T(8,128)(2,1)S(1)} all-to-all(bf16[16,80,640]{2,1,0:T(8,128)(2,1)S(1)} %shard_map.102), channel_id=1, replica_groups=mesh['clip'=4,'frame'=16,'mp'=4] {'frame'}, dimensions={0} | all-to-all | bytes 3276800 | tf_op jit(solution)/shard_map/all_to_all | solution.py:256
  47.6 0.0 copy-done.3
  47.6 0.0 copy-done.4
  47.6 9.4 %shard_map.103 = (bf16[640,640]{1,0:T(8,128)(2,1)}, bf16[16,416,128]{2,1,0:T(8,128)(2,1)S(1)}) custom-call(bf16[16,80,640]{2,1,0:T(8,128)(2,1)S(1)} %all_to_all.10.rc_ref, bf16[640,640]{1,0:T(8,128)(2,1)S(1)} %bitcast.22, f32[3,640]{1,0:T(4,128)S(1)} %copy-done.4), custom_call_target="tpu_custom_call" | custom-call | flops 16000000 | bytes 48000000 | tf_op jit(solution)/shard_map/pallas_call | solution.py:300
  57.0 25.7 %all_to_all.11.rc_ref = bf16[16,416,128]{2,1,0:T(8,128)(2,1)S(1)} all-to-all(bf16[16,416,128]{2,1,0:T(8,128)(2,1)S(1)} %get-tuple-element.20), channel_id=1, replica_groups=mesh['clip'=4,'frame'=16,'mp'=4] {'frame'}, dimensions={0} | all-to-all | bytes 3407872 | tf_op jit(solution)/shard_map/all_to_all | solution.py:256
  82.7 0.0 copy-start
  82.7 0.0 copy-start.1
  82.7 0.0 copy-start.2
  82.7 1.5 %shard_map.104 = (f32[16,40,640]{2,1,0:T(8,128)S(1)}, f32[1,640]{1,0:T(1,128)S(1)}, f32[3,640]{1,0:T(4,128)S(1)}) custom-call(s32[16]{0:T(128)S(1)} %bitcast.24, bf16[16,416,128]{2,1,0:T(8,128)(2,1)S(1)} %all_to_all.11.rc_ref, bf16[16,40,640]{2,1,0:T(8,128)(2,1)S(1)} %bitcast.14), custom_call_target="tpu_custom_call" | custom-call | flops 2000000 | bytes 6000000 | tf_op jit(solution)/shard_map/pallas_call | solution.py:311
  84.3 1.1 collective-permute-start.4
  85.3 2.6 %collective-permute-done.4 = f32[3,640]{1,0:T(4,128)S(1)} collective-permute-done((f32[3,640]{1,0:T(4,128)S(1)}, f32[3,640]{1,0:T(4,128)S(1)}, u32[]{:S(2)}, u32[]{:S(2)}) %collective-permute-start.4) | collective-permute-done | bytes 7712 | tf_op jit(solution)/shard_map/ppermute | solution.py:246
  88.0 1.5 %collective-permute-start.5 = (f32[3,640]{1,0:T(4,128)S(1)}, f32[3,640]{1,0:T(4,128)S(1)}, u32[]{:S(2)}, u32[]{:S(2)}) collective-permute-start(f32[3,640]{1,0:T(4,128)S(1)} %add.14), channel_id=1, source_target_pairs={{0,128},{64,192},{128,0},{192,64},{1,129},{65,193},{129,1},{193,65... | collective-permute-start | bytes 23048 | tf_op jit(solution)/shard_map/ppermute | solution.py:246
  89.5 0.0 collective-permute-start.2
  89.5 1.2 %collective-permute-done.2 = f32[1,640]{1,0:T(1,128)S(1)} collective-permute-done((f32[1,640]{1,0:T(1,128)S(1)}, f32[1,640]{1,0:T(1,128)S(1)}, u32[]{:S(2)}, u32[]{:S(2)}) %collective-permute-start.2) | collective-permute-done | bytes 2592 | tf_op jit(solution)/shard_map/ppermute | solution.py:246
  90.7 5.4 %collective-permute-start.3 = (f32[1,640]{1,0:T(1,128)S(1)}, f32[1,640]{1,0:T(1,128)S(1)}, u32[]{:S(2)}, u32[]{:S(2)}) collective-permute-start(f32[1,640]{1,0:T(1,128)S(1)} %add.13.i1_ref), channel_id=1, source_target_pairs={{0,2},{1,3},{2,0},{3,1},{4,6},{5,7},{6,4},{7,5},{8,10},{9,11},{10,... | collective-permute-start | bytes 7688 | tf_op jit(solution)/shard_map/ppermute | solution.py:246
  96.0 2.1 %collective-permute-done.3.i2_ref = f32[1,640]{1,0:T(1,128)S(1)} collective-permute-done((f32[1,640]{1,0:T(1,128)S(1)}, f32[1,640]{1,0:T(1,128)S(1)}, u32[]{:S(2)}, u32[]{:S(2)}) %collective-permute-start.3) | collective-permute-done | bytes 2592 | tf_op jit(solution)/shard_map/ppermute | solution.py:246
  98.2 0.0 copy-done
  98.2 0.0 copy-done.1
  98.2 0.0 copy-done.2
  98.2 6.5 %shard_map.105 = (bf16[640,640]{1,0:T(8,128)(2,1)}, bf16[640,640]{1,0:T(8,128)(2,1)}, bf16[640,640]{1,0:T(8,128)(2,1)}) custom-call(bf16[640,640]{1,0:T(8,128)(2,1)S(1)} %bitcast.16, bf16[640,640]{1,0:T(8,128)(2,1)S(1)} %bitcast.18, bf16[640,640]{1,0:T(8,128)(2,1)S(1)} %bitcast.20, bf16[5,640,640]{2,1,0:T(8,128)(2,1)S(1)} %get-tuple-element.19.p_ref, ...), custom_call_target="tpu_custom_call" | custom-call | flops 9000000 | bytes 27000000 | tf_op jit(solution)/shard_map/pallas_call | solution.py:324
  104.6 0.0 collective-permute-done.5
  104.6 0.6 add.15
  (3 shorter events, 0.0 us)
Async XLA Ops:
  0.6 17.2 %copy-start.5 = (s32[1,1,16]{2,1,0:T(1,128)S(1)}, s32[1,1,16]{2,1,0:T(1,128)}, u32[]{:S(2)}) copy-start(s32[1,1,16]{2,1,0:T(1,128)} %param.10) | copy-start | bytes 196
  7.8 1.3 %collective-permute-start = (f32[1,640]{1,0:T(1,128)S(1)}, f32[1,640]{1,0:T(1,128)S(1)}, u32[]{:S(2)}, u32[]{:S(2)}) collective-permute-start(f32[1,640]{1,0:T(1,128)S(1)} %get-tuple-element.17), channel_id=1, source_target_pairs={{0,1},{1,0},{2,3},{3,2},{4,5},{5,4},{6,7},{7,6},{8,9},{9,8},{10,11... | collective-permute-start | bytes 7688 | tf_op jit(solution)/shard_map/ppermute | solution.py:246
  9.1 8.8 %collective-permute-start.1 = (f32[1,640]{1,0:T(1,128)S(1)}, f32[1,640]{1,0:T(1,128)S(1)}, u32[]{:S(2)}, u32[]{:S(2)}) collective-permute-start(f32[1,640]{1,0:T(1,128)S(1)} %add.12.one_ref.s1_ref), channel_id=1, source_target_pairs={{0,2},{1,3},{2,0},{3,1},{4,6},{5,7},{6,4},{7,5},{8,10},{9,11},{10,... | collective-permute-start | bytes 7688 | tf_op jit(solution)/shard_map/ppermute | solution.py:246
  18.6 28.9 %copy-start.3 = (bf16[1,16,1,40,640]{4,3,2,1,0:T(8,128)(2,1)S(1)}, bf16[1,16,1,40,640]{4,3,2,1,0:T(8,128)(2,1)}, u32[]{:S(2)}) copy-start(bf16[1,16,1,40,640]{4,3,2,1,0:T(8,128)(2,1)} %param.11) | copy-start | bytes 2457604
  18.7 28.9 %copy-start.4 = (f32[3,640]{1,0:T(4,128)S(1)}, f32[3,640]{1,0:T(4,128)}, u32[]{:S(2)}) copy-start(f32[3,640]{1,0:T(4,128)} %gain_ref.1) | copy-start | bytes 23044
  82.7 15.4 %copy-start = (bf16[1,1,16,40,640]{4,3,2,1,0:T(8,128)(2,1)S(1)}, bf16[1,1,16,40,640]{4,3,2,1,0:T(8,128)(2,1)}, u32[]{:S(2)}) copy-start(bf16[1,1,16,40,640]{4,3,2,1,0:T(8,128)(2,1)} %param.6) | copy-start | bytes 2457604
  82.7 15.4 %copy-start.1 = (bf16[1,1,16,40,640]{4,3,2,1,0:T(8,128)(2,1)S(1)}, bf16[1,1,16,40,640]{4,3,2,1,0:T(8,128)(2,1)}, u32[]{:S(2)}) copy-start(bf16[1,1,16,40,640]{4,3,2,1,0:T(8,128)(2,1)} %param.7) | copy-start | bytes 2457604
  82.7 15.4 %copy-start.2 = (bf16[1,1,16,40,640]{4,3,2,1,0:T(8,128)(2,1)S(1)}, bf16[1,1,16,40,640]{4,3,2,1,0:T(8,128)(2,1)}, u32[]{:S(2)}) copy-start(bf16[1,1,16,40,640]{4,3,2,1,0:T(8,128)(2,1)} %param.8) | copy-start | bytes 2457604
  84.3 3.7 %collective-permute-start.4 = (f32[3,640]{1,0:T(4,128)S(1)}, f32[3,640]{1,0:T(4,128)S(1)}, u32[]{:S(2)}, u32[]{:S(2)}) collective-permute-start(f32[3,640]{1,0:T(4,128)S(1)} %get-tuple-element.26), channel_id=1, source_target_pairs={{0,64},{64,0},{128,192},{192,128},{1,65},{65,1},{129,193},{193,129... | collective-permute-start | bytes 23048 | tf_op jit(solution)/shard_map/ppermute | solution.py:246
  88.0 16.7 %collective-permute-start.5 = (f32[3,640]{1,0:T(4,128)S(1)}, f32[3,640]{1,0:T(4,128)S(1)}, u32[]{:S(2)}, u32[]{:S(2)}) collective-permute-start(f32[3,640]{1,0:T(4,128)S(1)} %add.14), channel_id=1, source_target_pairs={{0,128},{64,192},{128,0},{192,64},{1,129},{65,193},{129,1},{193,65... | collective-permute-start | bytes 23048 | tf_op jit(solution)/shard_map/ppermute | solution.py:246
  89.5 1.2 %collective-permute-start.2 = (f32[1,640]{1,0:T(1,128)S(1)}, f32[1,640]{1,0:T(1,128)S(1)}, u32[]{:S(2)}, u32[]{:S(2)}) collective-permute-start(f32[1,640]{1,0:T(1,128)S(1)} %get-tuple-element.22), channel_id=1, source_target_pairs={{0,1},{1,0},{2,3},{3,2},{4,5},{5,4},{6,7},{7,6},{8,9},{9,8},{10,11... | collective-permute-start | bytes 7688 | tf_op jit(solution)/shard_map/ppermute | solution.py:246
  90.7 7.5 %collective-permute-start.3 = (f32[1,640]{1,0:T(1,128)S(1)}, f32[1,640]{1,0:T(1,128)S(1)}, u32[]{:S(2)}, u32[]{:S(2)}) collective-permute-start(f32[1,640]{1,0:T(1,128)S(1)} %add.13.i1_ref), channel_id=1, source_target_pairs={{0,2},{1,3},{2,0},{3,1},{4,6},{5,7},{6,4},{7,5},{8,10},{9,11},{10,... | collective-permute-start | bytes 7688 | tf_op jit(solution)/shard_map/ppermute | solution.py:246

commit v5 on v4

--- a/solution.py
+++ b/solution.py
@@ -159,10 +159,15 @@
     dq = ds[...]
     normed = rc_ref[:, :TT, lanes(h)].astype(F32).reshape(TOK, HD)
     warped = rc_ref[:, TT:, lanes(h)].astype(F32).reshape(TOK, HD)
-    start = pl.multiple_of(h * 2 * TT, 16)
-    send_ref[:, pl.ds(start, TT), :] = (dq * gq).reshape(TILES, TT, HD).astype(BF16)
-    start = pl.multiple_of(start + TT, 8)
-    send_ref[:, pl.ds(start, TT), :] = (dk * gk + dv * gv).reshape(TILES, TT, HD).astype(BF16)
+    direct = (dq * gq).reshape(TILES, TT, HD).astype(BF16)
+    moved = (dk * gk + dv * gv).reshape(TILES, TT, HD).astype(BF16)
+    for n in range(HERE):
+
+        @pl.when(h == n)
+        def _(n=n):
+            send_ref[:, 2 * n * TT : (2 * n + 1) * TT, :] = direct
+            send_ref[:, (2 * n + 1) * TT : (2 * n + 2) * TT, :] = moved
+
     terms[0:1, lanes(h)] = column_sum(dq * normed)
     terms[1:2, lanes(h)] = column_sum(dk * warped)
     terms[2:3, lanes(h)] = column_sum(dv * warped)

time: 107 us -> 107 us (level)
  no operation moved by 1% of the time
where the time goes in v5:
time: 107 us; the launch traced here: 106 us
  blocking collectives  54.6 us (51%)
  Pallas kernels  26.3 us (25%)
  starting transfers between devices  15.2 us (14%)
  waiting for transfers between devices  8.64 us (8%)
    all_to_all x2, blocking collectives, exchanged(): return lax.all_to_all(x, 'frame', 0, 0, tiled=True)  54.6 us
    ppermute x6, starting transfers between devices, swapped(): return lax.ppermute(x, axis, [(i, i ^ flip) for i in range(size)])  15.2 us
    pallas_call x1, Pallas kernels, body(): call(temporal, heads, [held] * 3, [columns(), held], [flat, sds((TILES, H...  10.3 us
    ppermute x6, waiting for transfers between devices, swapped(): return lax.ppermute(x, axis, [(i, i ^ flip) for i in range(size)])  8.64 us
    pallas_call x1, Pallas kernels, body(): call(spatial_forward, heads, [away] * 3, [held] * 3, [flat, sds((HERE, TO...  7.15 us
    pallas_call x1, Pallas kernels, body(): call(spatial_backward, heads, [held] * 10, [columns()] * 3, [flat] * 3, [...  6.47 us
  transfers between devices with their start and end apart: 6, of which 5 were waited for; matrix products, arithmetic and copies ran while one was open for 0% of the time, Pallas kernels for 6%

profile of v5, /device:TPU:8, one launch (start us, length us, event | category | flops | bytes accessed | tf_op | source)
XLA Modules:
  0.0 106.1 jit_solution(553077369664465460)
XLA Ops:
  0.6 0.0 copy-start.5
  0.6 7.2 %shard_map.101 = (bf16[640,640]{1,0:T(8,128)(2,1)S(1)}, bf16[5,640,640]{2,1,0:T(8,128)(2,1)S(1)}, f32[1,640]{1,0:T(1,128)S(1)}) custom-call(bf16[640,640]{1,0:T(8,128)(2,1)} %bitcast.15, bf16[640,640]{1,0:T(8,128)(2,1)} %bitcast.17, bf16[640,640]{1,0:T(8,128)(2,1)} %bitcast.19), custom_call_target="tpu_custom_call" | custom-call | flops 7000000 | bytes 21000000 | tf_op jit(solution)/shard_map/pallas_call | solution.py:282
  7.8 0.1 collective-permute-start
  7.9 1.2 %collective-permute-done = f32[1,640]{1,0:T(1,128)S(1)} collective-permute-done((f32[1,640]{1,0:T(1,128)S(1)}, f32[1,640]{1,0:T(1,128)S(1)}, u32[]{:S(2)}, u32[]{:S(2)}) %collective-permute-start) | collective-permute-done | bytes 2592 | tf_op jit(solution)/shard_map/ppermute | solution.py:251
  9.1 7.2 %collective-permute-start.1 = (f32[1,640]{1,0:T(1,128)S(1)}, f32[1,640]{1,0:T(1,128)S(1)}, u32[]{:S(2)}, u32[]{:S(2)}) collective-permute-start(f32[1,640]{1,0:T(1,128)S(1)} %add.12.one_ref.s1_ref), channel_id=1, source_target_pairs={{0,2},{1,3},{2,0},{3,1},{4,6},{5,7},{6,4},{7,5},{8,10},{9,11},{10,... | collective-permute-start | bytes 7688 | tf_op jit(solution)/shard_map/ppermute | solution.py:251
  16.2 1.6 %collective-permute-done.1.two_ref.s2_ref = f32[1,640]{1,0:T(1,128)S(1)} collective-permute-done((f32[1,640]{1,0:T(1,128)S(1)}, f32[1,640]{1,0:T(1,128)S(1)}, u32[]{:S(2)}, u32[]{:S(2)}) %collective-permute-start.1) | collective-permute-done | bytes 2592 | tf_op jit(solution)/shard_map/ppermute | solution.py:251
  17.8 0.0 copy-done.5
  17.8 0.8 shard_map.102
  18.6 0.0 copy-start.3
  18.7 0.0 copy-start.4
  18.7 28.9 %all_to_all.10.rc_ref = bf16[16,80,640]{2,1,0:T(8,128)(2,1)S(1)} all-to-all(bf16[16,80,640]{2,1,0:T(8,128)(2,1)S(1)} %shard_map.102), channel_id=1, replica_groups=mesh['clip'=4,'frame'=16,'mp'=4] {'frame'}, dimensions={0} | all-to-all | bytes 3276800 | tf_op jit(solution)/shard_map/all_to_all | solution.py:261
  47.6 0.0 copy-done.3
  47.6 0.0 copy-done.4
  47.6 10.3 %shard_map.103 = (bf16[640,640]{1,0:T(8,128)(2,1)}, bf16[16,416,128]{2,1,0:T(8,128)(2,1)S(1)}) custom-call(bf16[16,80,640]{2,1,0:T(8,128)(2,1)S(1)} %all_to_all.10.rc_ref, bf16[640,640]{1,0:T(8,128)(2,1)S(1)} %bitcast.22, f32[3,640]{1,0:T(4,128)S(1)} %copy-done.4), custom_call_target="tpu_custom_call" | custom-call | flops 16000000 | bytes 48000000 | tf_op jit(solution)/shard_map/pallas_call | solution.py:305
  57.9 25.7 %all_to_all.11.rc_ref = bf16[16,416,128]{2,1,0:T(8,128)(2,1)S(1)} all-to-all(bf16[16,416,128]{2,1,0:T(8,128)(2,1)S(1)} %get-tuple-element.20), channel_id=1, replica_groups=mesh['clip'=4,'frame'=16,'mp'=4] {'frame'}, dimensions={0} | all-to-all | bytes 3407872 | tf_op jit(solution)/shard_map/all_to_all | solution.py:261
  83.6 0.0 copy-start
  83.6 0.0 copy-start.1
  83.6 0.0 copy-start.2
  83.6 1.5 %shard_map.104 = (f32[16,40,640]{2,1,0:T(8,128)S(1)}, f32[1,640]{1,0:T(1,128)S(1)}, f32[3,640]{1,0:T(4,128)S(1)}) custom-call(s32[16]{0:T(128)S(1)} %bitcast.24, bf16[16,416,128]{2,1,0:T(8,128)(2,1)S(1)} %all_to_all.11.rc_ref, bf16[16,40,640]{2,1,0:T(8,128)(2,1)S(1)} %bitcast.14), custom_call_target="tpu_custom_call" | custom-call | flops 2000000 | bytes 6000000 | tf_op jit(solution)/shard_map/pallas_call | solution.py:316
  85.1 1.0 collective-permute-start.4
  86.2 2.7 %collective-permute-done.4 = f32[3,640]{1,0:T(4,128)S(1)} collective-permute-done((f32[3,640]{1,0:T(4,128)S(1)}, f32[3,640]{1,0:T(4,128)S(1)}, u32[]{:S(2)}, u32[]{:S(2)}) %collective-permute-start.4) | collective-permute-done | bytes 7712 | tf_op jit(solution)/shard_map/ppermute | solution.py:251
  88.8 1.5 %collective-permute-start.5 = (f32[3,640]{1,0:T(4,128)S(1)}, f32[3,640]{1,0:T(4,128)S(1)}, u32[]{:S(2)}, u32[]{:S(2)}) collective-permute-start(f32[3,640]{1,0:T(4,128)S(1)} %add.14), channel_id=1, source_target_pairs={{0,128},{64,192},{128,0},{192,64},{1,129},{65,193},{129,1},{193,65... | collective-permute-start | bytes 23048 | tf_op jit(solution)/shard_map/ppermute | solution.py:251
  90.4 0.0 collective-permute-start.2
  90.4 1.2 %collective-permute-done.2 = f32[1,640]{1,0:T(1,128)S(1)} collective-permute-done((f32[1,640]{1,0:T(1,128)S(1)}, f32[1,640]{1,0:T(1,128)S(1)}, u32[]{:S(2)}, u32[]{:S(2)}) %collective-permute-start.2) | collective-permute-done | bytes 2592 | tf_op jit(solution)/shard_map/ppermute | solution.py:251
  91.5 5.4 %collective-permute-start.3 = (f32[1,640]{1,0:T(1,128)S(1)}, f32[1,640]{1,0:T(1,128)S(1)}, u32[]{:S(2)}, u32[]{:S(2)}) collective-permute-start(f32[1,640]{1,0:T(1,128)S(1)} %add.13.i1_ref), channel_id=1, source_target_pairs={{0,2},{1,3},{2,0},{3,1},{4,6},{5,7},{6,4},{7,5},{8,10},{9,11},{10,... | collective-permute-start | bytes 7688 | tf_op jit(solution)/shard_map/ppermute | solution.py:251
  96.9 2.1 %collective-permute-done.3.i2_ref = f32[1,640]{1,0:T(1,128)S(1)} collective-permute-done((f32[1,640]{1,0:T(1,128)S(1)}, f32[1,640]{1,0:T(1,128)S(1)}, u32[]{:S(2)}, u32[]{:S(2)}) %collective-permute-start.3) | collective-permute-done | bytes 2592 | tf_op jit(solution)/shard_map/ppermute | solution.py:251
  99.0 0.0 copy-done
  99.0 0.0 copy-done.1
  99.0 0.0 copy-done.2
  99.0 6.5 %shard_map.105 = (bf16[640,640]{1,0:T(8,128)(2,1)}, bf16[640,640]{1,0:T(8,128)(2,1)}, bf16[640,640]{1,0:T(8,128)(2,1)}) custom-call(bf16[640,640]{1,0:T(8,128)(2,1)S(1)} %bitcast.16, bf16[640,640]{1,0:T(8,128)(2,1)S(1)} %bitcast.18, bf16[640,640]{1,0:T(8,128)(2,1)S(1)} %bitcast.20, bf16[5,640,640]{2,1,0:T(8,128)(2,1)S(1)} %get-tuple-element.19.p_ref, ...), custom_call_target="tpu_custom_call" | custom-call | flops 9000000 | bytes 27000000 | tf_op jit(solution)/shard_map/pallas_call | solution.py:329
  105.5 0.0 collective-permute-done.5
  105.5 0.6 add.15
  (3 shorter events, 0.0 us)
Async XLA Ops:
  0.6 17.2 %copy-start.5 = (s32[1,1,16]{2,1,0:T(1,128)S(1)}, s32[1,1,16]{2,1,0:T(1,128)}, u32[]{:S(2)}) copy-start(s32[1,1,16]{2,1,0:T(1,128)} %param.10) | copy-start | bytes 196
  7.8 1.3 %collective-permute-start = (f32[1,640]{1,0:T(1,128)S(1)}, f32[1,640]{1,0:T(1,128)S(1)}, u32[]{:S(2)}, u32[]{:S(2)}) collective-permute-start(f32[1,640]{1,0:T(1,128)S(1)} %get-tuple-element.17), channel_id=1, source_target_pairs={{0,1},{1,0},{2,3},{3,2},{4,5},{5,4},{6,7},{7,6},{8,9},{9,8},{10,11... | collective-permute-start | bytes 7688 | tf_op jit(solution)/shard_map/ppermute | solution.py:251
  9.1 8.8 %collective-permute-start.1 = (f32[1,640]{1,0:T(1,128)S(1)}, f32[1,640]{1,0:T(1,128)S(1)}, u32[]{:S(2)}, u32[]{:S(2)}) collective-permute-start(f32[1,640]{1,0:T(1,128)S(1)} %add.12.one_ref.s1_ref), channel_id=1, source_target_pairs={{0,2},{1,3},{2,0},{3,1},{4,6},{5,7},{6,4},{7,5},{8,10},{9,11},{10,... | collective-permute-start | bytes 7688 | tf_op jit(solution)/shard_map/ppermute | solution.py:251
  18.6 28.9 %copy-start.3 = (bf16[1,16,1,40,640]{4,3,2,1,0:T(8,128)(2,1)S(1)}, bf16[1,16,1,40,640]{4,3,2,1,0:T(8,128)(2,1)}, u32[]{:S(2)}) copy-start(bf16[1,16,1,40,640]{4,3,2,1,0:T(8,128)(2,1)} %param.11) | copy-start | bytes 2457604
  18.7 28.9 %copy-start.4 = (f32[3,640]{1,0:T(4,128)S(1)}, f32[3,640]{1,0:T(4,128)}, u32[]{:S(2)}) copy-start(f32[3,640]{1,0:T(4,128)} %gain_ref.1) | copy-start | bytes 23044
  83.6 15.4 %copy-start = (bf16[1,1,16,40,640]{4,3,2,1,0:T(8,128)(2,1)S(1)}, bf16[1,1,16,40,640]{4,3,2,1,0:T(8,128)(2,1)}, u32[]{:S(2)}) copy-start(bf16[1,1,16,40,640]{4,3,2,1,0:T(8,128)(2,1)} %param.6) | copy-start | bytes 2457604
  83.6 15.4 %copy-start.1 = (bf16[1,1,16,40,640]{4,3,2,1,0:T(8,128)(2,1)S(1)}, bf16[1,1,16,40,640]{4,3,2,1,0:T(8,128)(2,1)}, u32[]{:S(2)}) copy-start(bf16[1,1,16,40,640]{4,3,2,1,0:T(8,128)(2,1)} %param.7) | copy-start | bytes 2457604
  83.6 15.4 %copy-start.2 = (bf16[1,1,16,40,640]{4,3,2,1,0:T(8,128)(2,1)S(1)}, bf16[1,1,16,40,640]{4,3,2,1,0:T(8,128)(2,1)}, u32[]{:S(2)}) copy-start(bf16[1,1,16,40,640]{4,3,2,1,0:T(8,128)(2,1)} %param.8) | copy-start | bytes 2457604
  85.1 3.7 %collective-permute-start.4 = (f32[3,640]{1,0:T(4,128)S(1)}, f32[3,640]{1,0:T(4,128)S(1)}, u32[]{:S(2)}, u32[]{:S(2)}) collective-permute-start(f32[3,640]{1,0:T(4,128)S(1)} %get-tuple-element.26), channel_id=1, source_target_pairs={{0,64},{64,0},{128,192},{192,128},{1,65},{65,1},{129,193},{193,129... | collective-permute-start | bytes 23048 | tf_op jit(solution)/shard_map/ppermute | solution.py:251
  88.8 16.7 %collective-permute-start.5 = (f32[3,640]{1,0:T(4,128)S(1)}, f32[3,640]{1,0:T(4,128)S(1)}, u32[]{:S(2)}, u32[]{:S(2)}) collective-permute-start(f32[3,640]{1,0:T(4,128)S(1)} %add.14), channel_id=1, source_target_pairs={{0,128},{64,192},{128,0},{192,64},{1,129},{65,193},{129,1},{193,65... | collective-permute-start | bytes 23048 | tf_op jit(solution)/shard_map/ppermute | solution.py:251
  90.4 1.2 %collective-permute-start.2 = (f32[1,640]{1,0:T(1,128)S(1)}, f32[1,640]{1,0:T(1,128)S(1)}, u32[]{:S(2)}, u32[]{:S(2)}) collective-permute-start(f32[1,640]{1,0:T(1,128)S(1)} %get-tuple-element.22), channel_id=1, source_target_pairs={{0,1},{1,0},{2,3},{3,2},{4,5},{5,4},{6,7},{7,6},{8,9},{9,8},{10,11... | collective-permute-start | bytes 7688 | tf_op jit(solution)/shard_map/ppermute | solution.py:251
  91.5 7.5 %collective-permute-start.3 = (f32[1,640]{1,0:T(1,128)S(1)}, f32[1,640]{1,0:T(1,128)S(1)}, u32[]{:S(2)}, u32[]{:S(2)}) collective-permute-start(f32[1,640]{1,0:T(1,128)S(1)} %add.13.i1_ref), channel_id=1, source_target_pairs={{0,2},{1,3},{2,0},{3,1},{4,6},{5,7},{6,4},{7,5},{8,10},{9,11},{10,... | collective-permute-start | bytes 7688 | tf_op jit(solution)/shard_map/ppermute | solution.py:251
